TPU v7x, 32 devices: a whole 2x2x4 slice. The times are simulated.
32 devices in a mesh: ty: 4 (over x, core), tx: 8 (over z, y).
Axes of the slice: x: 2, y: 2, z: 4, core: 2. Of those that a mesh axis runs over, the one named last changes fastest.
Arguments:
- tiles: bfloat16 [4, 8, 4, 512, 512], P('ty', 'tx'), may hold values from -6 to 6
- shifts: int32 [4, 8, 2], P('ty', 'tx'), may hold values from -28 to 28
- piece_target: int32 [4, 8, 256], P('ty', 'tx'), may hold values from 0 to 2047, as said below
- coarse_target: int32 [4, 8, 64], P('ty', 'tx'), may hold values from 0 to 511, as said below
Outputs:
- joined: bfloat16 [2048, 4096], P(('ty', 'tx'))
- coarse: bfloat16 [512, 256], P(('ty', 'tx'))
- corr_right: float32 [48, 1024], P('ty', 'tx')
- corr_below: float32 [48, 1024], P('ty', 'tx')
Inputs may be any that keep to these rules, and one draw needn't show every extreme that they name: `piece_target`: each tile sends at most 16 sub-blocks to the sub-blocks of one owner device; in every draw some owner devices receive exactly 16 from every tile. `coarse_target`: owners lie in the same tile row; every device sends exactly 8 pieces to each device of its row, and every target of every device is named exactly once.
All inputs are finite; a program needn't handle non-finite values.
Results may differ from a plain program's by a relative error of at most 0.008.
Values may be sent and summed in bfloat16 or wider, within the bound.
A program may use at most 128 MiB of HBM per device.

v0:
```python
import functools
import math

import jax
import jax.numpy as jnp
from jax import lax
from jax.experimental import pallas as pl
from jax.experimental.pallas import tpu as pltpu
from jax.sharding import PartitionSpec as P

SIDE = 32
OV = 48
H = 8
SLOTS = 64
LANES = 128
GROUPS = LANES // SIDE
F32 = jnp.float32
BF16 = jnp.bfloat16


def shifted(value, axis, steps):
    count = lax.axis_size(axis)
    first, last = (max(0, -steps), min(count, count - steps))
    return lax.ppermute(value, axis, [(source, source + steps) for source in range(first, last)])


def highest(left, right):
    return jnp.dot(left, right, precision=lax.Precision.HIGHEST, preferred_element_type=F32)


def iota(shape, dim):
    return lax.broadcasted_iota(jnp.int32, shape, dim)


def mm(a, b):
    return jnp.dot(a, b, preferred_element_type=F32)


def mm_t(a, b):
    return lax.dot_general(a, b, (((1,), (1,)), ((), ())), preferred_element_type=F32)


def bins_kernel(tile_ref, right_ref, left_ref, bottom_ref, top_ref):
    depth, length, _ = tile_ref.shape
    bins = OV // 4
    scale = 1.0 / math.sqrt(16.0 * depth)
    pool = (iota((length, length // 4), 0) // 4 == iota((length, length // 4), 1)).astype(F32)
    first = (iota((16, LANES), 1) // 4 == iota((16, LANES), 0)).astype(BF16)
    last = ((iota((16, LANES), 1) - (LANES - OV)) // 4 == iota((16, LANES), 0)) & (
        iota((16, LANES), 1) >= LANES - OV
    )
    last = last.astype(BF16)
    left = right = top = bottom = jnp.zeros((16, length), F32)
    for z in range(depth):
        left += mm_t(first, tile_ref[z, :, :LANES])
        right += mm_t(last, tile_ref[z, :, length - LANES :])
        top += mm(first, tile_ref[z, :LANES, :])
        bottom += mm(last, tile_ref[z, length - LANES :, :])
    for ref, value in ((right_ref, right), (left_ref, left), (bottom_ref, bottom), (top_ref, top)):
        ref[...] = highest(value, pool)[:bins] * scale


def all_bins(tile):
    length = tile.shape[1]
    shape = jax.ShapeDtypeStruct((OV // 4, length // 4), F32)
    vmem = pl.BlockSpec(memory_space=pltpu.VMEM)
    return pl.pallas_call(
        bins_kernel,
        out_shape=[shape] * 4,
        in_specs=[vmem],
        out_specs=[vmem] * 4,
        name="bins",
        cost_estimate=pl.CostEstimate(flops=10**8, bytes_accessed=2**21, transcendentals=0),
    )(tile)


def dft_tables(length):
    index = jnp.arange(length, dtype=jnp.int32)
    product = index[:, None] * index[None, :] % length
    angle = product.astype(F32) * (2.0 * math.pi / length)
    norm = 1.0 / math.sqrt(length)
    return (jnp.cos(angle) * norm, jnp.sin(angle) * norm)


def phase_kernel(ca_ref, sa_ref, cb_ref, sb_ref, r_ref, l_ref, b_ref, t_ref, right_ref, below_ref):
    cos_a, sin_a, cos_b, sin_b = ca_ref[...], sa_ref[...], cb_ref[...], sb_ref[...]

    def spectrum(values):
        left_cos = highest(cos_a, values)
        left_sin = highest(sin_a, values)
        re = highest(left_cos, cos_b) - highest(left_sin, sin_b)
        im = -(highest(left_cos, sin_b) + highest(left_sin, cos_b))
        return (re, im)

    for own_ref, other_ref, out_ref in ((r_ref, l_ref, right_ref), (b_ref, t_ref, below_ref)):
        own_re, own_im = spectrum(own_ref[...])
        other_re, other_im = spectrum(other_ref[...])
        cross_re = own_re * other_re + own_im * other_im
        cross_im = own_im * other_re - own_re * other_im
        scale = 1.0 / jnp.sqrt(cross_re * cross_re + cross_im * cross_im + 1.0)
        normed_re = cross_re * scale
        normed_im = cross_im * scale
        out = highest(highest(cos_a, normed_re) - highest(sin_a, normed_im), cos_b)
        out = out - highest(highest(sin_a, normed_re) + highest(cos_a, normed_im), sin_b)
        out_ref[...] = out


def phase_surfaces(right, left, bottom, top):
    rows, columns = right.shape
    pad = 16 - rows
    cos_a, sin_a = (jnp.pad(t, ((0, pad), (0, pad))) for t in dft_tables(rows))
    cos_b, sin_b = dft_tables(columns)
    padded = [jnp.pad(v, ((0, pad), (0, 0))) for v in (right, left, bottom, top)]
    vmem = pl.BlockSpec(memory_space=pltpu.VMEM)
    out = pl.pallas_call(
        phase_kernel,
        out_shape=[jax.ShapeDtypeStruct((16, columns), F32)] * 2,
        in_specs=[vmem] * 8,
        out_specs=[vmem] * 2,
        name="phase",
        cost_estimate=pl.CostEstimate(flops=10**8, bytes_accessed=2**18, transcendentals=4096),
    )(cos_a, sin_a, cos_b, sin_b, *padded)
    return out[0][:rows], out[1][:rows]


def swap_groups(parts):
    group = iota(parts[0].shape, 1) // SIDE

    def pick(choices):
        value = choices[3]
        for g in range(3):
            value = jnp.where(group == g, choices[g], value)
        return value

    turned = []
    for d in range(GROUPS):
        mixed = pick([parts[(g + d) % GROUPS] for g in range(GROUPS)])
        turned.append(pltpu.roll(mixed, d * SIDE, 1) if d else mixed)
    return [pick([turned[(j - g) % GROUPS] for j in range(GROUPS)]) for g in range(GROUPS)]


def taps(offset, shape, out_dim, column):
    whole, frac = offset
    at = iota(shape, out_dim) + whole + H
    return (
        jnp.where(column == at, 1.0 - frac, 0.0) + jnp.where(column == at + 1, frac, 0.0)
    ).astype(BF16)


def split_shift(shift):
    whole = lax.shift_right_arithmetic(shift, 2)
    return whole, (shift - 4 * whole).astype(F32) * 0.25


def ramp(shape, dim, length):
    index = iota(shape, dim)
    nearest = jnp.minimum(jnp.minimum(index + 1, length - index), OV).astype(F32)
    return 1.0 + 3.0 * nearest / OV


def pieces_kernel(shift_ref, pos_ref, tile_ref, tb_ref, side_ref, corner_ref, send_ref, work_ref):
    depth, length, _ = tile_ref.shape

    def edge_column(shape, dim):
        c = iota(shape, dim)
        return jnp.where(c < H, c, c + length)

    sy, sx = split_shift(shift_ref[0]), split_shift(shift_ref[1])
    full, thin, wide = (length, length), (length, 2 * H), (2 * H, length)
    ry = taps(sy, full, 0, iota(full, 1) + H)
    ry_edge = taps(sy, thin, 0, edge_column(thin, 1))
    rx = taps(sx, full, 1, iota(full, 0) + H)
    rx_edge = taps(sx, wide, 1, edge_column(wide, 0))
    weights = ramp((length, 1), 0, length) * ramp((1, length), 1, length)
    for z in range(depth):
        along = (mm(ry, tile_ref[z]) + mm(ry_edge, tb_ref[z])).astype(BF16)
        along_side = (mm_t(ry, side_ref[z]) + mm_t(ry_edge, corner_ref[z])).astype(BF16)
        resampled = mm(along, rx) + mm(along_side, rx_edge)
        work_ref[z] = weights * resampled
    send_ref[...] = jnp.zeros_like(send_ref)
    grid_side = length // SIDE

    def row(py, carry):
        start = pl.multiple_of(py * SIDE, SIDE)
        for q in range(length // LANES):
            parts = [work_ref[z, pl.ds(start, SIDE), q * LANES : (q + 1) * LANES] for z in range(depth)]
            for g, piece in enumerate(swap_groups(parts)):
                send_ref[pos_ref[py * grid_side + q * GROUPS + g]] = piece.astype(BF16)
        return carry

    lax.fori_loop(0, grid_side, row, 0)


def make_pieces(shifts, position, tile, tb, side, corner, rows):
    vmem = pl.BlockSpec(memory_space=pltpu.VMEM)
    smem = pl.BlockSpec(memory_space=pltpu.SMEM)
    return pl.pallas_call(
        pieces_kernel,
        out_shape=jax.ShapeDtypeStruct((rows, SIDE, LANES), BF16),
        in_specs=[smem, smem, vmem, vmem, vmem, vmem],
        out_specs=vmem,
        scratch_shapes=[pltpu.VMEM(tile.shape, F32)],
        name="pieces",
        compiler_params=pltpu.CompilerParams(vmem_limit_bytes=40 * 2**20),
        cost_estimate=pl.CostEstimate(flops=2 * 10**9, bytes_accessed=2**23, transcendentals=0),
    )(shifts, position, tile, tb, side, corner)


def join_kernel(slot_ref, got_ref, denom_ref, joined_ref, quads_ref, acc_ref, mean_ref):
    acc_ref[...] = jnp.zeros_like(acc_ref)

    def add(i, carry):
        slot = slot_ref[i]

        @pl.when(slot < SLOTS)
        def _():
            acc_ref[slot] = acc_ref[slot] + got_ref[i].astype(F32)

        return carry

    lax.fori_loop(0, got_ref.shape[0], add, 0, unroll=4)
    row = iota((LANES, LANES), 0)
    column = iota((LANES, LANES), 1)
    half = SIDE // 2
    pool_one = ((row // (2 * SIDE)) * half + (row % SIDE) // 2 == column).astype(BF16)
    pool_two = (((row % half) // 2 == column) & (row < SIDE)).astype(BF16)

    def finish(s, carry):
        value = (acc_ref[s] / jnp.maximum(denom_ref[s], 1.0)).astype(BF16)
        acc_ref[s] = value.astype(F32)
        mean_ref[...] = mm(value, pool_one)
        level = (mean_ref[pl.ds(0, half, stride=2), :] + mean_ref[pl.ds(1, half, stride=2), :]) * 0.125
        mean_ref[pl.ds(0, half), :] = mm(level.astype(BF16), pool_two)
        quads_ref[s] = (
            mean_ref[pl.ds(0, half // 2, stride=2), :] + mean_ref[pl.ds(1, half // 2, stride=2), :]
        ) * 0.125
        return carry

    lax.fori_loop(0, SLOTS, finish, 0, unroll=2)

    def restore(s, carry):
        rows = SIDE // GROUPS
        parts = [acc_ref[s, pl.ds(j, rows, stride=GROUPS), :] for j in range(GROUPS)]
        joined_ref[s] = jnp.concatenate(swap_groups(parts), axis=0).astype(BF16)
        return carry

    lax.fori_loop(0, SLOTS, restore, 0, unroll=2)


def join(slots, got, denom):
    vmem = pl.BlockSpec(memory_space=pltpu.VMEM)
    smem = pl.BlockSpec(memory_space=pltpu.SMEM)
    return pl.pallas_call(
        join_kernel,
        out_shape=[
            jax.ShapeDtypeStruct((SLOTS, SIDE, LANES), BF16),
            jax.ShapeDtypeStruct((SLOTS, SIDE // 4, LANES), F32),
        ],
        in_specs=[smem, vmem, vmem],
        out_specs=[vmem, vmem],
        scratch_shapes=[pltpu.VMEM((SLOTS, SIDE, LANES), F32), pltpu.VMEM((SIDE, LANES), F32)],
        name="join",
        compiler_params=pltpu.CompilerParams(vmem_limit_bytes=32 * 2**20),
        cost_estimate=pl.CostEstimate(flops=10**8, bytes_accessed=2**23, transcendentals=0),
    )(slots, got, denom)


def assemble(quadrant_blocks):
    count, height, width = quadrant_blocks.shape
    shaped = quadrant_blocks.reshape(count // 4, 2, 2, height, width).transpose(0, 1, 3, 2, 4)
    return shaped.reshape(count // 4, 4 * height * width)


def patch_weights(length, depth):
    grid_side = length // SIDE
    index = jnp.arange(length, dtype=jnp.int32)
    nearest = jnp.minimum(jnp.minimum(index + 1, length - index), OV).astype(F32)
    line = (1.0 + 3.0 * nearest / OV).reshape(grid_side, SIDE)
    across = jnp.tile(line, (1, depth))
    blend = line[:, None, :, None] * across[None, :, None, :]
    return blend.astype(BF16).reshape(grid_side * grid_side, SIDE * depth * SIDE)


def per_device(tiles, shifts, piece_target, coarse_target):
    tile = tiles[0, 0]
    count_y = lax.axis_size("ty")
    count_x = lax.axis_size("tx")
    devices = count_y * count_x
    depth, length, _ = tile.shape
    pieces_n = (length // SIDE) ** 2
    capacity = 2 * pieces_n // devices
    me = lax.axis_index("ty") * count_x + lax.axis_index("tx")

    top = shifted(tile[:, length - H :, :], "ty", 1)
    bottom = shifted(tile[:, :H, :], "ty", -1)
    targets = piece_target[0, 0]
    owners = targets // SLOTS
    order = jnp.arange(pieces_n, dtype=jnp.int32)
    earlier = (owners[:, None] == owners[None, :]) & (order[None, :] < order[:, None])
    position = owners * capacity + jnp.sum(earlier.astype(jnp.int32), axis=1)
    gathered = lax.all_gather(targets, ("ty", "tx"))

    tb = jnp.concatenate([top, bottom], axis=1)
    last = jnp.concatenate([tile[:, :, length - H :], tb[:, :, length - H :]], axis=1)
    first = jnp.concatenate([tile[:, :, :H], tb[:, :, :H]], axis=1)
    left = shifted(last.transpose(0, 2, 1), "tx", 1)
    right = shifted(first.transpose(0, 2, 1), "tx", -1)
    side = jnp.concatenate([left, right], axis=1)
    send = make_pieces(
        shifts[0, 0], position, tile, tb, side[:, :, :length], side[:, :, length:], devices * capacity
    )
    got = lax.all_to_all(send, ("ty", "tx"), split_axis=0, concat_axis=0, tiled=True)

    right_bins, left_bins, bottom_bins, top_bins = all_bins(tile)
    next_left = shifted(left_bins, "tx", -1)
    next_top = shifted(top_bins, "ty", -1)
    corr_right, corr_below = phase_surfaces(right_bins, next_left, bottom_bins, next_top)

    mine = gathered // SLOTS == me
    local = gathered % SLOTS
    marks = mine.astype(jnp.int32)
    rank = jnp.cumsum(marks, axis=1) - marks
    chosen = mine[:, None, :] & (rank[:, None, :] == jnp.arange(capacity, dtype=jnp.int32)[None, :, None])
    slots = SLOTS + jnp.sum(jnp.where(chosen, local[:, None, :] - SLOTS, 0), axis=2)
    wanted = me * SLOTS + jnp.arange(SLOTS, dtype=jnp.int32)
    counts = jnp.sum((gathered[None] == wanted[:, None, None]).astype(F32), axis=1).astype(BF16)
    denom = mm(counts, patch_weights(length, depth)).reshape(SLOTS, SIDE, LANES)

    joined, quads = join(slots.reshape(-1), got, denom)
    joined = joined.reshape(SLOTS, depth * SIDE * SIDE)

    coarse_ids = coarse_target[0, 0]
    owner = coarse_ids // SLOTS
    per_peer = SLOTS // count_x
    number = jnp.arange(SLOTS, dtype=jnp.int32)
    ahead = (owner[:, None] == owner[None, :]) & (number[None, :] < number[:, None])
    coarse_pos = owner * per_peer + jnp.sum(ahead.astype(jnp.int32), axis=1)
    ordering = (coarse_pos[None, :] == number[:, None])
    send_local = jnp.sum(jnp.where(ordering, (coarse_ids % SLOTS)[None, :], 0), axis=1)
    got_local = lax.all_to_all(send_local, "tx", split_axis=0, concat_axis=0, tiled=True)
    flat = quads[:, :, : SIDE // 4].astype(BF16).reshape(SLOTS, -1)
    send_quads = mm(ordering.astype(BF16), flat).astype(BF16)
    got_quads = lax.all_to_all(send_quads, "tx", split_axis=0, concat_axis=0, tiled=True)
    place = (got_local[None, :] == number[:, None]).astype(BF16)
    placed = mm(place, got_quads).reshape(SLOTS, SIDE // 4, SIDE // 4)
    coarse = assemble(placed).astype(BF16)
    return (joined, coarse, corr_right, corr_below)


def solution(mesh):
    placed = (
        P("ty", "tx", None, None, None),
        P("ty", "tx", None),
        P("ty", "tx", None),
        P("ty", "tx", None),
    )
    return jax.shard_map(
        per_device,
        mesh=mesh,
        in_specs=placed,
        out_specs=(P(("ty", "tx"), None), P(("ty", "tx"), None), P("ty", "tx"), P("ty", "tx")),
        check_vma=False,
    )
```

profile of v0, /device:TPU:0, one launch (start us, length us, event | category | flops | bytes accessed | tf_op | source)
XLA Modules:
  0.0 240.6 jit_solution(8950459540049088063)
XLA Ops:
  0.6 0.0 copy-start
  0.7 0.9 fusion.32
  1.6 2.3 collective-permute-start
  3.9 1.3 collective-permute-start.1
  5.2 1.4 fusion.31
  6.7 0.2 convert_reduce_fusion.1
  6.9 0.2 copy.39
  7.1 0.2 copy.41
  7.3 1.9 collective-permute-done.1
  9.2 0.1 fusion.33
  9.2 0.1 copy.40
  9.3 3.4 %collective-permute-start.2 = (bf16[4,8,528]{2,1,0:T(8,128)(2,1)S(1)}, bf16[4,8,528]{2,1,0:T(8,128)(2,1)S(1)}, u32[]{:S(2)}, u32[]{:S(2)}) collective-permute-start(bf16[4,8,528]{2,1,0:T(8,128)(2,1)S(1)} %maximum_bitcast_fusion), channel_id=1, source_target_pairs={{0,1},{1,2},{2,3},{3,4},{4,5},{5,6},{6,7},{8,9},{9,10},{10,11},{11... | collective-permute-start | bytes 101384 | tf_op jit(solution)/shard_map/ppermute | solution.py:24
  12.8 0.1 copy.42
  12.9 1.3 collective-permute-start.3
  14.2 0.3 collective-permute-done.2
  14.4 4.3 %collective-permute-done.3 = bf16[4,8,528]{2,1,0:T(8,128)(2,1)S(1)} collective-permute-done((bf16[4,8,528]{2,1,0:T(8,128)(2,1)S(1)}, bf16[4,8,528]{2,1,0:T(8,128)(2,1)S(1)}, u32[]{:S(2)}, u32[]{:S(2)}) %collective-permute-start.3) | collective-permute-done | bytes 33824 | tf_op jit(solution)/shard_map/ppermute | solution.py:24
  18.8 7.1 %pieces.1 = bf16[512,32,128]{2,1,0:T(8,128)(2,1)S(1)} custom-call(s32[2]{0:T(128)S(1)} %bitcast.89, s32[256]{0:T(256)S(1)} %multiply_add_fusion.2.pos_ref, bf16[4,512,512]{2,1,0:T(8,128)(2,1)S(1)} %bitcast.87, bf16[4,16,512]{2,1,0:T(8,128)(2,1)S(1)} %constant_dynamic-update-slice_fusion.tb_ref, bf16[4,16,512]{2,1,0:T(8,128)(2,1)S(1)} %slice.60.side_ref, ...), custom_call_target="tpu_custom_call" | custom-call | flops 2000000000 | bytes 8388608 | tf_op jit(solution)/shard_map/pieces/pallas_call | solution.py:197
  26.0 2.0 copy-done.1
  27.9 7.4 %all-to-all-start = ((bf16[512,32,128]{2,1,0:T(8,128)(2,1)}), bf16[512,32,128]{2,1,0:T(8,128)(2,1)}, u32[]{:S(2)}, u32[]{:S(2)}) async-start(bf16[512,32,128]{2,1,0:T(8,128)(2,1)} %copy-done.1), calls=%async_computation | async-start | bytes 8388608 | tf_op jit(solution)/shard_map/all_to_all | solution.py:312
  35.3 3.2 %bins.1 = (f32[12,128]{1,0:T(8,128)}, f32[12,128]{1,0:T(8,128)}, f32[12,128]{1,0:T(8,128)}, f32[12,128]{1,0:T(8,128)}) custom-call(bf16[4,512,512]{2,1,0:T(8,128)(2,1)} %bitcast.86), custom_call_target="tpu_custom_call" | custom-call | flops 100000000 | bytes 2097152 | tf_op jit(solution)/shard_map/bins/pallas_call | solution.py:67
  38.5 1.3 collective-permute-start.4
  39.8 1.3 collective-permute-start.5
  41.1 143.2 %all-gather = s32[32,1,256]{2,1,0:T(1,128)S(1)} all-gather(s32[1,1,256]{2,1,0:T(1,128)S(1)} %copy-done.3), channel_id=2, replica_groups=mesh['ty'=4,'tx'=8] {'ty','tx'}, dimensions={0}, use_global_device_ids=true | all-gather | bytes 33792 | tf_op jit(solution)/shard_map/all_gather | solution.py:301
  184.4 0.6 reduce-window.6
  185.0 0.2 slice_reduce_fusion
  185.2 0.1 convert_subtract_fusion
  185.3 0.6 select_reduce_fusion
  185.9 0.1 add.155.slot_ref
  186.0 0.1 tile.8
  186.1 0.4 multiply_convert_fusion
  186.5 2.4 copy.68
  188.9 3.3 %copy.52 = bf16[4096,256]{1,0:T(8,128)(2,1)S(1)} copy(bf16[4096,256]{0,1:T(8,128)(2,1)} %bitcast.92) | data formatting | bytes 4194304 | tf_op jit(solution)/shard_map/dot_general | solution.py:36
  192.2 0.4 convert_reduce_fusion
  192.6 0.0 copy-start.6
  192.6 0.7 fusion.12
  193.3 0.6 copy.44.denom_ref
  194.0 0.2 convert_reduce_fusion.2
  194.2 0.1 select_reduce_fusion.1
  194.3 0.7 all_to_all.18
  195.0 0.1 cosine_multiply_fusion.1
  195.0 0.1 sine_multiply_fusion.1
  195.1 0.9 sine_multiply_fusion
  196.0 3.3 %all-to-all-start.1 = ((s32[8,8,1]{1,2,0:T(1,128)}), s32[8,8,1]{1,2,0:T(1,128)S(1)}, u32[]{:S(2)}, u32[]{:S(2)}) async-start(s32[8,8,1]{1,2,0:T(1,128)} %bitcast.9), calls=%async_computation.1 | async-start | bytes 8192 | tf_op jit(solution)/shard_map/all_to_all | solution.py:340
  199.3 0.0 copy-start.5
  199.3 23.4 %join.1 = (bf16[64,32,128]{2,1,0:T(8,128)(2,1)S(1)}, f32[64,8,128]{2,1,0:T(8,128)S(1)}) custom-call(s32[512]{0:T(512)S(1)} %add.155.slot_ref, bf16[512,32,128]{2,1,0:T(8,128)(2,1)} %all-to-all-done.got_ref, f32[64,32,128]{2,1,0:T(8,128)S(1)} %copy.44.denom_ref), custom_call_target="tpu_custom_call" | custom-call | flops 100000000 | bytes 8388608 | tf_op jit(solution)/shard_map/join/pallas_call | solution.py:253
  222.7 0.1 copy.46
  222.9 0.1 fusion.1
  223.0 0.7 reshape.274
  223.7 5.9 %all-to-all-start.2 = ((bf16[8,2,256]{2,1,0:T(2,128)(2,1)}), bf16[8,2,256]{2,1,0:T(2,128)(2,1)S(1)}, u32[]{:S(2)}, u32[]{:S(2)}) async-start(bf16[8,2,256]{2,1,0:T(2,128)(2,1)} %reshape.274), calls=%async_computation.2 | async-start | bytes 16384 | tf_op jit(solution)/shard_map/all_to_all | solution.py:343
  229.6 0.6 pad.22.r_ref
  230.3 0.6 pad.24.b_ref
  230.9 0.6 pad.20.ca_ref
  231.5 0.6 pad.21.sa_ref
  232.0 0.5 broadcast.373
  232.6 0.7 reduce.5
  233.2 0.1 eq.111
  233.3 0.6 pad.23.l_ref
  233.9 0.6 pad.25.t_ref
  234.5 3.9 %phase.1 = (f32[16,128]{1,0:T(8,128)}, f32[16,128]{1,0:T(8,128)}) custom-call(f32[16,16]{1,0:T(8,128)} %pad.20.ca_ref, f32[16,16]{1,0:T(8,128)} %pad.21.sa_ref, f32[128,128]{1,0:T(8,128)} %get-tuple-element.45.cb_ref, f32[128,128]{1,0:T(8,128)} %get-tuple-element.44.sb_ref, f32[16,128]{1,0:T(8,128)} %pad.22.r_ref, f32[16,128]{1,0:T(8,128)} %pad.23.l_ref, ...), custom_call_target="tpu_custom_call" | custom-call | flops 100000000 | bytes 262144 | tf_op jit(solution)/shard_map/phase/pallas_call | solution.py:115
  238.5 1.0 copy.69
  239.5 0.1 reshape.275
  239.5 0.1 copy.47
  239.6 0.3 fusion
  239.9 0.7 copy.49
  (40 shorter events, 0.3 us)
Async XLA Ops:
  0.6 18.2 %copy-start = (bf16[1,1,4,512,512]{4,3,2,1,0:T(8,128)(2,1)S(1)}, bf16[1,1,4,512,512]{4,3,2,1,0:T(8,128)(2,1)}, u32[]{:S(2)}) copy-start(bf16[1,1,4,512,512]{4,3,2,1,0:T(8,128)(2,1)} %param.4) | copy-start | bytes 6291460
  0.6 6.0 %copy-start.3 = (s32[1,1,256]{2,1,0:T(1,128)S(1)}, s32[1,1,256]{2,1,0:T(1,128)}, u32[]{:S(2)}) copy-start(s32[1,1,256]{2,1,0:T(1,128)} %param.6) | copy-start | bytes 3076
  0.7 18.1 %copy-start.2 = (s32[1,1,2]{2,1,0:T(1,128)S(1)}, s32[1,1,2]{2,1,0:T(1,128)}, u32[]{:S(2)}) copy-start(s32[1,1,2]{2,1,0:T(1,128)} %param.5) | copy-start | bytes 28
  1.6 5.7 %collective-permute-start = (bf16[4,8,512]{2,1,0:T(8,128)(2,1)S(1)}, bf16[4,8,512]{2,1,0:T(8,128)(2,1)S(1)}, u32[]{:S(2)}, u32[]{:S(2)}) collective-permute-start(bf16[4,8,512]{2,1,0:T(8,128)(2,1)S(1)} %get-tuple-element.37), channel_id=1, source_target_pairs={{0,8},{8,16},{16,24},{1,9},{9,17},{17,25},{2,10},{10,18},{18,26},{... | collective-permute-start | bytes 98312 | tf_op jit(solution)/shard_map/ppermute | solution.py:24
  3.9 5.2 %collective-permute-start.1 = (bf16[4,8,512]{2,1,0:T(8,128)(2,1)S(1)}, bf16[4,8,512]{2,1,0:T(8,128)(2,1)S(1)}, u32[]{:S(2)}, u32[]{:S(2)}) collective-permute-start(bf16[4,8,512]{2,1,0:T(8,128)(2,1)S(1)} %get-tuple-element.36), channel_id=1, source_target_pairs={{8,0},{16,8},{24,16},{9,1},{17,9},{25,17},{10,2},{18,10},{26,18},{... | collective-permute-start | bytes 98312 | tf_op jit(solution)/shard_map/ppermute | solution.py:24
  9.3 5.1 %collective-permute-start.2 = (bf16[4,8,528]{2,1,0:T(8,128)(2,1)S(1)}, bf16[4,8,528]{2,1,0:T(8,128)(2,1)S(1)}, u32[]{:S(2)}, u32[]{:S(2)}) collective-permute-start(bf16[4,8,528]{2,1,0:T(8,128)(2,1)S(1)} %maximum_bitcast_fusion), channel_id=1, source_target_pairs={{0,1},{1,2},{2,3},{3,4},{4,5},{5,6},{6,7},{8,9},{9,10},{10,11},{11... | collective-permute-start | bytes 101384 | tf_op jit(solution)/shard_map/ppermute | solution.py:24
  12.9 5.9 %collective-permute-start.3 = (bf16[4,8,528]{2,1,0:T(8,128)(2,1)S(1)}, bf16[4,8,528]{2,1,0:T(8,128)(2,1)S(1)}, u32[]{:S(2)}, u32[]{:S(2)}) collective-permute-start(bf16[4,8,528]{2,1,0:T(8,128)(2,1)S(1)} %maximum_bitcast_fusion.1), channel_id=1, source_target_pairs={{1,0},{2,1},{3,2},{4,3},{5,4},{6,5},{7,6},{9,8},{10,9},{11,10},{12... | collective-permute-start | bytes 101384 | tf_op jit(solution)/shard_map/ppermute | solution.py:24
  26.0 2.0 copy-start.1
  27.9 168.1 %all-to-all-start = ((bf16[512,32,128]{2,1,0:T(8,128)(2,1)}), bf16[512,32,128]{2,1,0:T(8,128)(2,1)}, u32[]{:S(2)}, u32[]{:S(2)}) async-start(bf16[512,32,128]{2,1,0:T(8,128)(2,1)} %copy-done.1), calls=%async_computation | async-start | bytes 8388608 | tf_op jit(solution)/shard_map/all_to_all | solution.py:312
  38.5 194.8 %collective-permute-start.4 = (f32[12,128]{1,0:T(8,128)}, f32[12,128]{1,0:T(8,128)S(1)}, u32[]{:S(2)}, u32[]{:S(2)}) collective-permute-start(f32[12,128]{1,0:T(8,128)} %get-tuple-element.15), channel_id=1, source_target_pairs={{1,0},{2,1},{3,2},{4,3},{5,4},{6,5},{7,6},{9,8},{10,9},{11,10},{12... | collective-permute-start | bytes 18440 | tf_op jit(solution)/shard_map/ppermute | solution.py:24
  39.8 194.1 %collective-permute-start.5 = (f32[12,128]{1,0:T(8,128)}, f32[12,128]{1,0:T(8,128)S(1)}, u32[]{:S(2)}, u32[]{:S(2)}) collective-permute-start(f32[12,128]{1,0:T(8,128)} %get-tuple-element.17), channel_id=1, source_target_pairs={{8,0},{16,8},{24,16},{9,1},{17,9},{25,17},{10,2},{18,10},{26,18},{... | collective-permute-start | bytes 18440 | tf_op jit(solution)/shard_map/ppermute | solution.py:24
  192.6 1.4 copy-start.6
  196.0 27.7 %all-to-all-start.1 = ((s32[8,8,1]{1,2,0:T(1,128)}), s32[8,8,1]{1,2,0:T(1,128)S(1)}, u32[]{:S(2)}, u32[]{:S(2)}) async-start(s32[8,8,1]{1,2,0:T(1,128)} %bitcast.9), calls=%async_computation.1 | async-start | bytes 8192 | tf_op jit(solution)/shard_map/all_to_all | solution.py:340
  199.3 30.3 %copy-start.5 = (f32[12,128]{1,0:T(8,128)S(1)}, f32[12,128]{1,0:T(8,128)}, u32[]{:S(2)}) copy-start(f32[12,128]{1,0:T(8,128)} %get-tuple-element.14) | copy-start | bytes 18436
  199.3 30.9 %copy-start.4 = (f32[12,128]{1,0:T(8,128)S(1)}, f32[12,128]{1,0:T(8,128)}, u32[]{:S(2)}) copy-start(f32[12,128]{1,0:T(8,128)} %get-tuple-element.16) | copy-start | bytes 18436
  223.7 15.8 %all-to-all-start.2 = ((bf16[8,2,256]{2,1,0:T(2,128)(2,1)}), bf16[8,2,256]{2,1,0:T(2,128)(2,1)S(1)}, u32[]{:S(2)}, u32[]{:S(2)}) async-start(bf16[8,2,256]{2,1,0:T(2,128)(2,1)} %reshape.274), calls=%async_computation.2 | async-start | bytes 16384 | tf_op jit(solution)/shard_map/all_to_all | solution.py:343
where the time goes:
time: 241 us
  blocking collectives  143 us (59%)
  Pallas kernels  37.7 us (16%)
  starting transfers between devices  27.5 us (11%)
  local copies, waits for them, and re-layouts  19.2 us (8%)
  waiting for transfers between devices  6.46 us (3%)
  other arithmetic  4.44 us (2%)
    all_gather x1, blocking collectives, per_device(): gathered = lax.all_gather(targets, ('ty', 'tx'))  143 us
    pallas_call x1, Pallas kernels, join(): pl.pallas_call(join_kernel, out_shape=[jax.ShapeDtypeStruct((SLOTS, SIDE,...  23.4 us
    ppermute x6, starting transfers between devices, shifted(): lax.ppermute(value, axis, [(source, source + steps) for source in range(f...  10.9 us
    all_to_all x1, starting transfers between devices, per_device(): lax.all_to_all(send, ('ty', 'tx'), split_axis=0, concat_axis=0, tiled=True)  7.39 us
    pallas_call x1, Pallas kernels, make_pieces(): pl.pallas_call(pieces_kernel, out_shape=jax.ShapeDtypeStruct((rows, SIDE,...  7.15 us
    unnamed x22, local copies, waits for them, and re-layouts  6.84 us
    ppermute x6, waiting for transfers between devices, shifted(): lax.ppermute(value, axis, [(source, source + steps) for source in range(f...  6.45 us
    all_to_all x1, starting transfers between devices, per_device(): lax.all_to_all(send_quads, 'tx', split_axis=0, concat_axis=0, tiled=True)  5.93 us
  transfers between devices with their start and end apart: 9, of which 3 were waited for; matrix products, arithmetic and copies ran while one was open for 8% of the time, Pallas kernels for 13%

commit v1 on v0

--- a/solution.py
+++ b/solution.py
@@ -12,6 +12,7 @@
 OV = 48
 H = 8
 SLOTS = 64
+CODE = 2 * SLOTS
 LANES = 128
 GROUPS = LANES // SIDE
 F32 = jnp.float32
@@ -206,45 +207,38 @@
     )(shifts, position, tile, tb, side, corner)
 
 
-def join_kernel(slot_ref, got_ref, denom_ref, joined_ref, quads_ref, acc_ref, mean_ref):
+def join_kernel(slot_ref, got_ref, denom_ref, joined_ref, quads_ref, acc_ref, sum_ref, mean_ref):
     acc_ref[...] = jnp.zeros_like(acc_ref)
+    step = 8
 
     def add(i, carry):
-        slot = slot_ref[i]
-
-        @pl.when(slot < SLOTS)
-        def _():
-            acc_ref[slot] = acc_ref[slot] + got_ref[i].astype(F32)
-
+        for j in range(step):
+            slot = slot_ref[i * step + j]
+            acc_ref[slot] = acc_ref[slot] + got_ref[i * step + j].astype(F32)
         return carry
 
-    lax.fori_loop(0, got_ref.shape[0], add, 0, unroll=4)
+    lax.fori_loop(0, got_ref.shape[0] // step, add, 0)
     row = iota((LANES, LANES), 0)
     column = iota((LANES, LANES), 1)
     half = SIDE // 2
     pool_one = ((row // (2 * SIDE)) * half + (row % SIDE) // 2 == column).astype(BF16)
     pool_two = (((row % half) // 2 == column) & (row < SIDE)).astype(BF16)
-
-    def finish(s, carry):
-        value = (acc_ref[s] / jnp.maximum(denom_ref[s], 1.0)).astype(BF16)
-        acc_ref[s] = value.astype(F32)
-        mean_ref[...] = mm(value, pool_one)
-        level = (mean_ref[pl.ds(0, half, stride=2), :] + mean_ref[pl.ds(1, half, stride=2), :]) * 0.125
-        mean_ref[pl.ds(0, half), :] = mm(level.astype(BF16), pool_two)
-        quads_ref[s] = (
-            mean_ref[pl.ds(0, half // 2, stride=2), :] + mean_ref[pl.ds(1, half // 2, stride=2), :]
+    batch = SLOTS // 4
+    rows = batch * SIDE
+    for c in range(SLOTS // batch):
+        part = pl.ds(c * batch, batch)
+        value = (acc_ref[part] / jnp.maximum(denom_ref[part], 1.0)).astype(BF16).reshape(rows, LANES)
+        mean_ref[...] = value.astype(F32)
+        sum_ref[...] = mm(value, pool_one)
+        level = (sum_ref[pl.ds(0, rows // 2, stride=2), :] + sum_ref[pl.ds(1, rows // 2, stride=2), :]) * 0.125
+        sum_ref[pl.ds(0, rows // 2), :] = mm(level.astype(BF16), pool_two)
+        quads_ref[pl.ds(c * rows // 4, rows // 4), :] = (
+            sum_ref[pl.ds(0, rows // 4, stride=2), :] + sum_ref[pl.ds(1, rows // 4, stride=2), :]
         ) * 0.125
-        return carry
-
-    lax.fori_loop(0, SLOTS, finish, 0, unroll=2)
-
-    def restore(s, carry):
-        rows = SIDE // GROUPS
-        parts = [acc_ref[s, pl.ds(j, rows, stride=GROUPS), :] for j in range(GROUPS)]
-        joined_ref[s] = jnp.concatenate(swap_groups(parts), axis=0).astype(BF16)
-        return carry
-
-    lax.fori_loop(0, SLOTS, restore, 0, unroll=2)
+        parts = [mean_ref[pl.ds(j, rows // GROUPS, stride=GROUPS), :] for j in range(GROUPS)]
+        high = SIDE // GROUPS
+        for g, piece in enumerate(swap_groups(parts)):
+            joined_ref[part, pl.ds(g * high, high), :] = piece.reshape(batch, high, LANES).astype(BF16)
 
 
 def join(slots, got, denom):
@@ -254,11 +248,15 @@
         join_kernel,
         out_shape=[
             jax.ShapeDtypeStruct((SLOTS, SIDE, LANES), BF16),
-            jax.ShapeDtypeStruct((SLOTS, SIDE // 4, LANES), F32),
+            jax.ShapeDtypeStruct((SLOTS * SIDE // 4, LANES), F32),
         ],
         in_specs=[smem, vmem, vmem],
         out_specs=[vmem, vmem],
-        scratch_shapes=[pltpu.VMEM((SLOTS, SIDE, LANES), F32), pltpu.VMEM((SIDE, LANES), F32)],
+        scratch_shapes=[
+            pltpu.VMEM((SLOTS + 1, SIDE, LANES), F32),
+            pltpu.VMEM((SLOTS // 4 * SIDE, LANES), F32),
+            pltpu.VMEM((SLOTS // 4 * SIDE, LANES), F32),
+        ],
         name="join",
         compiler_params=pltpu.CompilerParams(vmem_limit_bytes=32 * 2**20),
         cost_estimate=pl.CostEstimate(flops=10**8, bytes_accessed=2**23, transcendentals=0),
@@ -289,45 +287,44 @@
     depth, length, _ = tile.shape
     pieces_n = (length // SIDE) ** 2
     capacity = 2 * pieces_n // devices
-    me = lax.axis_index("ty") * count_x + lax.axis_index("tx")
-
-    top = shifted(tile[:, length - H :, :], "ty", 1)
-    bottom = shifted(tile[:, :H, :], "ty", -1)
+
     targets = piece_target[0, 0]
     owners = targets // SLOTS
     order = jnp.arange(pieces_n, dtype=jnp.int32)
     earlier = (owners[:, None] == owners[None, :]) & (order[None, :] < order[:, None])
     position = owners * capacity + jnp.sum(earlier.astype(jnp.int32), axis=1)
-    gathered = lax.all_gather(targets, ("ty", "tx"))
-
+    codes = order * CODE + targets % SLOTS - SLOTS
+    rows = jnp.arange(devices * capacity, dtype=jnp.int32)
+    send_codes = SLOTS + jnp.sum(
+        jnp.where(position[None, :] == rows[:, None], codes[None, :], 0), axis=1
+    )
+    got_codes = lax.all_to_all(send_codes, ("ty", "tx"), split_axis=0, concat_axis=0, tiled=True)
+
+    top = shifted(tile[:, length - H :, :], "ty", 1)
+    bottom = shifted(tile[:, :H, :], "ty", -1)
     tb = jnp.concatenate([top, bottom], axis=1)
     last = jnp.concatenate([tile[:, :, length - H :], tb[:, :, length - H :]], axis=1)
     first = jnp.concatenate([tile[:, :, :H], tb[:, :, :H]], axis=1)
     left = shifted(last.transpose(0, 2, 1), "tx", 1)
     right = shifted(first.transpose(0, 2, 1), "tx", -1)
     side = jnp.concatenate([left, right], axis=1)
+    right_bins, left_bins, bottom_bins, top_bins = all_bins(tile)
+    position, got_codes, left_bins, top_bins = lax.optimization_barrier(
+        (position, got_codes, left_bins, top_bins)
+    )
+    next_left = shifted(left_bins, "tx", -1)
+    next_top = shifted(top_bins, "ty", -1)
     send = make_pieces(
         shifts[0, 0], position, tile, tb, side[:, :, :length], side[:, :, length:], devices * capacity
     )
     got = lax.all_to_all(send, ("ty", "tx"), split_axis=0, concat_axis=0, tiled=True)
 
-    right_bins, left_bins, bottom_bins, top_bins = all_bins(tile)
-    next_left = shifted(left_bins, "tx", -1)
-    next_top = shifted(top_bins, "ty", -1)
     corr_right, corr_below = phase_surfaces(right_bins, next_left, bottom_bins, next_top)
-
-    mine = gathered // SLOTS == me
-    local = gathered % SLOTS
-    marks = mine.astype(jnp.int32)
-    rank = jnp.cumsum(marks, axis=1) - marks
-    chosen = mine[:, None, :] & (rank[:, None, :] == jnp.arange(capacity, dtype=jnp.int32)[None, :, None])
-    slots = SLOTS + jnp.sum(jnp.where(chosen, local[:, None, :] - SLOTS, 0), axis=2)
-    wanted = me * SLOTS + jnp.arange(SLOTS, dtype=jnp.int32)
-    counts = jnp.sum((gathered[None] == wanted[:, None, None]).astype(F32), axis=1).astype(BF16)
+    slots = got_codes % CODE
+    slot_marks = slots[None, :] == jnp.arange(SLOTS, dtype=jnp.int32)[:, None]
+    place_marks = (got_codes // CODE)[:, None] == order[None, :]
+    counts = mm(slot_marks.astype(BF16), place_marks.astype(BF16)).astype(BF16)
     denom = mm(counts, patch_weights(length, depth)).reshape(SLOTS, SIDE, LANES)
-
-    joined, quads = join(slots.reshape(-1), got, denom)
-    joined = joined.reshape(SLOTS, depth * SIDE * SIDE)
 
     coarse_ids = coarse_target[0, 0]
     owner = coarse_ids // SLOTS
@@ -335,14 +332,20 @@
     number = jnp.arange(SLOTS, dtype=jnp.int32)
     ahead = (owner[:, None] == owner[None, :]) & (number[None, :] < number[:, None])
     coarse_pos = owner * per_peer + jnp.sum(ahead.astype(jnp.int32), axis=1)
-    ordering = (coarse_pos[None, :] == number[:, None])
-    send_local = jnp.sum(jnp.where(ordering, (coarse_ids % SLOTS)[None, :], 0), axis=1)
-    got_local = lax.all_to_all(send_local, "tx", split_axis=0, concat_axis=0, tiled=True)
-    flat = quads[:, :, : SIDE // 4].astype(BF16).reshape(SLOTS, -1)
-    send_quads = mm(ordering.astype(BF16), flat).astype(BF16)
+    ordering = (coarse_pos[None, :] == number[:, None]).astype(BF16)
+    locals_ = jnp.broadcast_to((coarse_ids % SLOTS).astype(BF16)[:, None], (SLOTS, SLOTS))
+    got, denom, slots, ordering, locals_, corr_right, corr_below = lax.optimization_barrier(
+        (got, denom, slots, ordering, locals_, corr_right, corr_below)
+    )
+    joined, quads = join(slots, got, denom)
+    joined = joined.reshape(SLOTS, depth * SIDE * SIDE)
+    flat = quads[:, : SIDE // 4].astype(BF16).reshape(SLOTS, -1)
+    send_quads = mm(ordering, jnp.concatenate([flat, locals_], axis=1)).astype(BF16)
     got_quads = lax.all_to_all(send_quads, "tx", split_axis=0, concat_axis=0, tiled=True)
+    width = flat.shape[1]
+    got_local = got_quads[:, width].astype(jnp.int32)
     place = (got_local[None, :] == number[:, None]).astype(BF16)
-    placed = mm(place, got_quads).reshape(SLOTS, SIDE // 4, SIDE // 4)
+    placed = mm(place, got_quads[:, :width]).reshape(SLOTS, SIDE // 4, SIDE // 4)
     coarse = assemble(placed).astype(BF16)
     return (joined, coarse, corr_right, corr_below)
 

time: 241 us -> 169 us (0.70)
  blocking collectives: 143 us -> 0 us
  waiting for transfers between devices: 6.46 us -> 82.7 us
  Pallas kernels: 37.7 us -> 20.5 us
  starting transfers between devices: 27.5 us -> 36.6 us
    all_gather x1 -> x0, blocking collectives: 143 us -> none  [per_device(): gathered = lax.all_gather(targets, ('ty', 'tx'))]
    all_to_all x1, waiting for transfers between devices: 0.01 us -> 67.8 us  [per_device(): lax.all_to_all(send, ('ty', 'tx'), split_axis=0, concat_axis=0, tiled=True)]
    pallas_call x1, Pallas kernels: 23.4 us -> 6.25 us  [join(): pl.pallas_call(join_kernel, out_shape=[jax.ShapeDtypeStruct((SLOTS, SIDE,...]
    all_to_all x1, waiting for transfers between devices: 0.01 us -> 5.57 us  [per_device(): lax.all_to_all(send_quads, 'tx', split_axis=0, concat_axis=0, tiled=True)]
    all_to_all x1, starting transfers between devices: 7.39 us -> 11.4 us  [per_device(): lax.all_to_all(send, ('ty', 'tx'), split_axis=0, concat_axis=0, tiled=True)]
    all_to_all x1, starting transfers between devices: 3.28 us -> 7.3 us  [per_device(): lax.all_to_all(send_codes, ('ty', 'tx'), split_axis=0, concat_axis=0, til...]
    ppermute x6, waiting for transfers between devices: 6.45 us -> 9.34 us  [shifted(): lax.ppermute(value, axis, [(source, source + steps) for source in range(f...]
    unnamed x22 -> x21, local copies, waits for them, and re-layouts: 6.84 us -> 8.82 us
  transfers between devices with their start and end apart: 9 -> 9, of which waited for: 3 -> 3; matrix products, arithmetic and copies ran while one was open for 8% -> 12% of each run, Pallas kernels for 13% -> 4%
where the time goes in v1:
time: 169 us; the launch traced here: 168 us
  waiting for transfers between devices  82.7 us (49%)
  starting transfers between devices  36.6 us (22%)
  local copies, waits for them, and re-layouts  20.8 us (12%)
  Pallas kernels  20.5 us (12%)
  other arithmetic  4.81 us (3%)
  matrix products  1.89 us (1%)
    all_to_all x1, waiting for transfers between devices, per_device(): lax.all_to_all(send, ('ty', 'tx'), split_axis=0, concat_axis=0, tiled=True)  67.8 us
    ppermute x6, starting transfers between devices, shifted(): lax.ppermute(value, axis, [(source, source + steps) for source in range(f...  12.1 us
    all_to_all x1, starting transfers between devices, per_device(): lax.all_to_all(send, ('ty', 'tx'), split_axis=0, concat_axis=0, tiled=True)  11.4 us
    ppermute x6, waiting for transfers between devices, shifted(): lax.ppermute(value, axis, [(source, source + steps) for source in range(f...  9.34 us
    unnamed x21, local copies, waits for them, and re-layouts  8.82 us
    all_to_all x1, starting transfers between devices, per_device(): lax.all_to_all(send_codes, ('ty', 'tx'), split_axis=0, concat_axis=0, til...  7.3 us
    pallas_call x1, Pallas kernels, make_pieces(): pl.pallas_call(pieces_kernel, out_shape=jax.ShapeDtypeStruct((rows, SIDE,...  7.16 us
    pallas_call x1, Pallas kernels, join(): pl.pallas_call(join_kernel, out_shape=[jax.ShapeDtypeStruct((SLOTS, SIDE,...  6.25 us
  transfers between devices with their start and end apart: 9, of which 3 were waited for; matrix products, arithmetic and copies ran while one was open for 12% of the time, Pallas kernels for 4%

profile of v1, /device:TPU:0, one launch (start us, length us, event | category | flops | bytes accessed | tf_op | source)
XLA Modules:
  0.0 168.3 jit_solution(11706382664225146159)
XLA Ops:
  0.6 0.7 fusion.30
  1.3 0.2 convert_reduce_fusion
  1.5 0.2 select_reduce_fusion
  1.7 0.7 add.166
  2.4 7.3 %all-to-all-start = ((s32[32,16,1]{1,2,0:T(1,128)}), s32[32,16,1]{1,2,0:T(1,128)S(1)}, u32[]{:S(2)}, u32[]{:S(2)}) async-start(s32[32,16,1]{1,2,0:T(1,128)} %bitcast.2), calls=%async_computation | async-start | bytes 32768 | tf_op jit(solution)/shard_map/all_to_all | solution.py:301
  9.7 2.8 %copy.44 = bf16[1,1,4,512,512]{3,4,2,1,0:T(8,128)(2,1)S(1)} copy(bf16[1,1,4,512,512]{4,3,2,1,0:T(8,128)(2,1)} %param.4) | data formatting | bytes 4194304 | tf_op args[0]
  12.5 1.2 fusion.34
  13.7 2.2 %collective-permute-start = (bf16[4,8,512]{1,2,0:T(8,128)(2,1)}, bf16[4,8,512]{1,2,0:T(8,128)(2,1)S(1)}, u32[]{:S(2)}, u32[]{:S(2)}) collective-permute-start(bf16[4,8,512]{1,2,0:T(8,128)(2,1)} %get-tuple-element.60), channel_id=1, source_target_pairs={{0,8},{8,16},{16,24},{1,9},{9,17},{17,25},{2,10},{10,18},{18,26},{... | collective-permute-start | bytes 98312 | tf_op jit(solution)/shard_map/ppermute | solution.py:25
  15.9 1.3 collective-permute-start.1
  17.2 3.2 %bins.1 = (f32[12,128]{1,0:T(8,128)}, f32[12,128]{1,0:T(8,128)}, f32[12,128]{1,0:T(8,128)}, f32[12,128]{1,0:T(8,128)}) custom-call(bf16[4,512,512]{2,1,0:T(8,128)(2,1)} %bitcast.52), custom_call_target="tpu_custom_call" | custom-call | flops 100000000 | bytes 2097152 | tf_op jit(solution)/shard_map/bins/pallas_call | solution.py:68
  20.4 0.0 all-to-all-done
  20.4 0.6 broadcast.428
  21.0 0.7 reduce.5
  21.7 0.1 all_to_all.18
  21.8 0.0 collective-permute-done
  21.8 0.0 collective-permute-done.1
  21.8 0.1 fusion.22
  21.9 1.3 collective-permute-start.3
  23.2 4.5 %collective-permute-start.2 = (bf16[4,8,528]{2,1,0:T(8,128)(2,1)S(1)}, bf16[4,8,528]{2,1,0:T(8,128)(2,1)S(1)}, u32[]{:S(2)}, u32[]{:S(2)}) collective-permute-start(bf16[4,8,528]{2,1,0:T(8,128)(2,1)S(1)} %maximum_bitcast_fusion), channel_id=1, source_target_pairs={{0,1},{1,2},{2,3},{3,4},{4,5},{5,6},{6,7},{8,9},{9,10},{10,11},{11... | collective-permute-start | bytes 101384 | tf_op jit(solution)/shard_map/ppermute | solution.py:25
  27.8 1.1 pad_maximum_fusion
  28.8 1.2 copy.47.tb_ref
  30.0 0.0 collective-permute-done.2
  30.1 0.0 collective-permute-done.3
  30.1 0.0 copy-done
  30.1 0.0 copy-done.2
  30.1 7.2 %pieces.1 = bf16[512,32,128]{2,1,0:T(8,128)(2,1)S(1)} custom-call(s32[2]{0:T(128)S(1)} %bitcast.55, s32[256]{0:T(256)S(1)} %multiply_add_fusion.1.pos_ref, bf16[4,512,512]{2,1,0:T(8,128)(2,1)S(1)} %bitcast.53, bf16[4,16,512]{2,1,0:T(8,128)(2,1)S(1)} %copy.47.tb_ref, bf16[4,16,512]{2,1,0:T(8,128)(2,1)S(1)} %slice.61.side_ref, ...), custom_call_target="tpu_custom_call" | custom-call | flops 2000000000 | bytes 8388608 | tf_op jit(solution)/shard_map/pieces/pallas_call | solution.py:198
  37.3 0.0 copy-start.1
  37.3 2.0 %copy-done.1 = bf16[512,32,128]{2,1,0:T(8,128)(2,1)} copy-done((bf16[512,32,128]{2,1,0:T(8,128)(2,1)}, bf16[512,32,128]{2,1,0:T(8,128)(2,1)S(1)}, u32[]{:S(2)}) %copy-start.1) | copy-done | bytes 4194328
  39.3 11.4 %all-to-all-start.1 = ((bf16[512,32,128]{2,1,0:T(8,128)(2,1)}), bf16[512,32,128]{2,1,0:T(8,128)(2,1)}, u32[]{:S(2)}, u32[]{:S(2)}) async-start(bf16[512,32,128]{2,1,0:T(8,128)(2,1)} %copy-done.1), calls=%async_computation.1 | async-start | bytes 8388608 | tf_op jit(solution)/shard_map/all_to_all | solution.py:320
  50.7 0.6 pad.22.r_ref
  51.3 0.0 copy-done.3
  51.3 0.6 pad.24.b_ref
  51.9 0.1 cosine_multiply_fusion.1
  52.0 0.6 pad.20.ca_ref
  52.6 0.1 sine_multiply_fusion.1
  52.7 0.6 pad.21.sa_ref
  53.3 0.1 tile.8
  53.4 0.4 multiply_convert_fusion
  53.8 2.4 %copy.59 = bf16[32,8,32,128]{3,1,2,0:T(8,128)(2,1)} copy(bf16[32,8,32,128]{3,2,1,0:T(8,128)(2,1)S(1)} %bitcast.57) | data formatting | bytes 4194304
  56.2 3.3 %copy.54 = bf16[4096,256]{1,0:T(8,128)(2,1)S(1)} copy(bf16[4096,256]{0,1:T(8,128)(2,1)} %bitcast.58) | data formatting | bytes 4194304 | tf_op jit(solution)/shard_map/dot_general | solution.py:37
  59.5 0.2 convert_reduce_fusion.2
  59.7 0.9 sine_multiply_fusion
  60.6 1.3 collective-permute-start.4
  61.9 1.5 collective-permute-start.5
  63.4 1.0 fusion.2
  64.4 9.3 %collective-permute-done.4 = f32[12,128]{1,0:T(8,128)S(1)} collective-permute-done((f32[12,128]{1,0:T(8,128)S(1)}, f32[12,128]{1,0:T(8,128)S(1)}, u32[]{:S(2)}, u32[]{:S(2)}) %collective-permute-start.4) | collective-permute-done | bytes 6176 | tf_op jit(solution)/shard_map/ppermute | solution.py:25
  73.7 0.6 pad.23.l_ref
  74.3 0.0 collective-permute-done.5
  74.3 0.6 pad.25.t_ref
  74.9 3.9 %phase.1 = (f32[16,128]{1,0:T(8,128)}, f32[16,128]{1,0:T(8,128)}) custom-call(f32[16,16]{1,0:T(8,128)} %pad.20.ca_ref, f32[16,16]{1,0:T(8,128)} %pad.21.sa_ref, f32[128,128]{1,0:T(8,128)} %get-tuple-element.71.cb_ref, f32[128,128]{1,0:T(8,128)} %get-tuple-element.70.sb_ref, f32[16,128]{1,0:T(8,128)} %pad.22.r_ref, f32[16,128]{1,0:T(8,128)} %pad.23.l_ref, ...), custom_call_target="tpu_custom_call" | custom-call | flops 100000000 | bytes 262144 | tf_op jit(solution)/shard_map/phase/pallas_call | solution.py:116
  78.9 67.8 %all-to-all-done.1.got_ref = bf16[512,32,128]{2,1,0:T(8,128)(2,1)} async-done(((bf16[512,32,128]{2,1,0:T(8,128)(2,1)}), bf16[512,32,128]{2,1,0:T(8,128)(2,1)}, u32[]{:S(2)}, u32[]{:S(2)}) %all-to-all-start.1) | async-done | bytes 4194336 | tf_op jit(solution)/shard_map/all_to_all | solution.py:320
  146.7 0.1 broadcast_in_dim.16
  146.8 0.6 copy.49.denom_ref
  147.4 6.2 %join.1 = (bf16[64,32,128]{2,1,0:T(8,128)(2,1)S(1)}, f32[512,128]{1,0:T(8,128)S(1)}) custom-call(s32[512]{0:T(512)S(1)} %get-tuple-element.33.slot_ref, bf16[512,32,128]{2,1,0:T(8,128)(2,1)} %all-to-all-done.1.got_ref, f32[64,32,128]{2,1,0:T(8,128)S(1)} %copy.49.denom_ref), custom_call_target="tpu_custom_call" | custom-call | flops 100000000 | bytes 8388608 | tf_op jit(solution)/shard_map/join/pallas_call | solution.py:247
  153.7 0.1 reshape.272
  153.8 0.8 fusion.1
  154.6 5.8 %all-to-all-start.2 = ((bf16[8,8,128]{2,1,0:T(8,128)(2,1)}), bf16[8,8,128]{2,1,0:T(8,128)(2,1)S(1)}, u32[]{:S(2)}, u32[]{:S(2)}) async-start(bf16[8,8,128]{2,1,0:T(8,128)(2,1)} %fusion.1), calls=%async_computation.2 | async-start | bytes 32768 | tf_op jit(solution)/shard_map/all_to_all | solution.py:344
  160.4 1.0 copy.60
  161.4 5.6 %all-to-all-done.2 = bf16[8,8,128]{2,1,0:T(8,128)(2,1)S(1)} async-done(((bf16[8,8,128]{2,1,0:T(8,128)(2,1)}), bf16[8,8,128]{2,1,0:T(8,128)(2,1)S(1)}, u32[]{:S(2)}, u32[]{:S(2)}) %all-to-all-start.2) | async-done | bytes 16416 | tf_op jit(solution)/shard_map/all_to_all | solution.py:344
  166.9 0.2 convert_reduce_fusion.1
  167.1 0.1 convolution_convert_fusion.1
  167.2 0.1 convert_element_type.98
  167.4 0.2 copy.50
  167.6 0.7 copy.51
  (27 shorter events, 0.2 us)
Async XLA Ops:
  2.4 18.0 %all-to-all-start = ((s32[32,16,1]{1,2,0:T(1,128)}), s32[32,16,1]{1,2,0:T(1,128)S(1)}, u32[]{:S(2)}, u32[]{:S(2)}) async-start(s32[32,16,1]{1,2,0:T(1,128)} %bitcast.2), calls=%async_computation | async-start | bytes 32768 | tf_op jit(solution)/shard_map/all_to_all | solution.py:301
  13.7 8.1 %collective-permute-start = (bf16[4,8,512]{1,2,0:T(8,128)(2,1)}, bf16[4,8,512]{1,2,0:T(8,128)(2,1)S(1)}, u32[]{:S(2)}, u32[]{:S(2)}) collective-permute-start(bf16[4,8,512]{1,2,0:T(8,128)(2,1)} %get-tuple-element.60), channel_id=1, source_target_pairs={{0,8},{8,16},{16,24},{1,9},{9,17},{17,25},{2,10},{10,18},{18,26},{... | collective-permute-start | bytes 98312 | tf_op jit(solution)/shard_map/ppermute | solution.py:25
  15.9 5.9 %collective-permute-start.1 = (bf16[4,8,512]{1,2,0:T(8,128)(2,1)}, bf16[4,8,512]{1,2,0:T(8,128)(2,1)S(1)}, u32[]{:S(2)}, u32[]{:S(2)}) collective-permute-start(bf16[4,8,512]{1,2,0:T(8,128)(2,1)} %get-tuple-element.61), channel_id=1, source_target_pairs={{8,0},{16,8},{24,16},{9,1},{17,9},{25,17},{10,2},{18,10},{26,18},{... | collective-permute-start | bytes 98312 | tf_op jit(solution)/shard_map/ppermute | solution.py:25
  20.4 9.8 %copy-start = (bf16[1,1,4,512,512]{4,3,2,1,0:T(8,128)(2,1)S(1)}, bf16[1,1,4,512,512]{4,3,2,1,0:T(8,128)(2,1)}, u32[]{:S(2)}) copy-start(bf16[1,1,4,512,512]{4,3,2,1,0:T(8,128)(2,1)} %param.4) | copy-start | bytes 6291460
  20.4 9.8 %copy-start.2 = (s32[1,1,2]{2,1,0:T(1,128)S(1)}, s32[1,1,2]{2,1,0:T(1,128)}, u32[]{:S(2)}) copy-start(s32[1,1,2]{2,1,0:T(1,128)} %param.5) | copy-start | bytes 28
  21.9 8.2 %collective-permute-start.3 = (bf16[4,8,528]{2,1,0:T(8,128)(2,1)S(1)}, bf16[4,8,528]{2,1,0:T(8,128)(2,1)S(1)}, u32[]{:S(2)}, u32[]{:S(2)}) collective-permute-start(bf16[4,8,528]{2,1,0:T(8,128)(2,1)S(1)} %maximum_bitcast_fusion.1), channel_id=1, source_target_pairs={{1,0},{2,1},{3,2},{4,3},{5,4},{6,5},{7,6},{9,8},{10,9},{11,10},{12... | collective-permute-start | bytes 101384 | tf_op jit(solution)/shard_map/ppermute | solution.py:25
  23.2 6.9 %collective-permute-start.2 = (bf16[4,8,528]{2,1,0:T(8,128)(2,1)S(1)}, bf16[4,8,528]{2,1,0:T(8,128)(2,1)S(1)}, u32[]{:S(2)}, u32[]{:S(2)}) collective-permute-start(bf16[4,8,528]{2,1,0:T(8,128)(2,1)S(1)} %maximum_bitcast_fusion), channel_id=1, source_target_pairs={{0,1},{1,2},{2,3},{3,4},{4,5},{5,6},{6,7},{8,9},{9,10},{10,11},{11... | collective-permute-start | bytes 101384 | tf_op jit(solution)/shard_map/ppermute | solution.py:25
  37.3 2.0 %copy-start.1 = (bf16[512,32,128]{2,1,0:T(8,128)(2,1)}, bf16[512,32,128]{2,1,0:T(8,128)(2,1)S(1)}, u32[]{:S(2)}) copy-start(bf16[512,32,128]{2,1,0:T(8,128)(2,1)S(1)} %pieces.1) | copy-start | bytes 12582916
  39.3 11.5 %copy-start.4 = (f32[12,128]{1,0:T(8,128)S(1)}, f32[12,128]{1,0:T(8,128)}, u32[]{:S(2)}) copy-start(f32[12,128]{1,0:T(8,128)} %get-tuple-element.27) | copy-start | bytes 18436
  39.3 12.1 %copy-start.3 = (f32[12,128]{1,0:T(8,128)S(1)}, f32[12,128]{1,0:T(8,128)}, u32[]{:S(2)}) copy-start(f32[12,128]{1,0:T(8,128)} %get-tuple-element.29) | copy-start | bytes 18436
  39.3 107.4 %all-to-all-start.1 = ((bf16[512,32,128]{2,1,0:T(8,128)(2,1)}), bf16[512,32,128]{2,1,0:T(8,128)(2,1)}, u32[]{:S(2)}, u32[]{:S(2)}) async-start(bf16[512,32,128]{2,1,0:T(8,128)(2,1)} %copy-done.1), calls=%async_computation.1 | async-start | bytes 8388608 | tf_op jit(solution)/shard_map/all_to_all | solution.py:320
  56.2 3.3 %copy-start.7 = (s32[1,1,64]{2,1,0:T(1,128)S(1)}, s32[1,1,64]{2,1,0:T(1,128)}, u32[]{:S(2)}) copy-start(s32[1,1,64]{2,1,0:T(1,128)} %param.7) | copy-start | bytes 772
  56.2 4.5 %copy-start.6 = (f32[12,128]{1,0:T(8,128)S(1)}, f32[12,128]{1,0:T(8,128)}, u32[]{:S(2)}) copy-start(f32[12,128]{1,0:T(8,128)} %get-tuple-element.28) | copy-start | bytes 18436
  56.2 5.8 %copy-start.5 = (f32[12,128]{1,0:T(8,128)S(1)}, f32[12,128]{1,0:T(8,128)}, u32[]{:S(2)}) copy-start(f32[12,128]{1,0:T(8,128)} %get-tuple-element.30) | copy-start | bytes 18436
  60.6 13.1 %collective-permute-start.4 = (f32[12,128]{1,0:T(8,128)S(1)}, f32[12,128]{1,0:T(8,128)S(1)}, u32[]{:S(2)}, u32[]{:S(2)}) collective-permute-start(f32[12,128]{1,0:T(8,128)S(1)} %copy-done.6), channel_id=1, source_target_pairs={{1,0},{2,1},{3,2},{4,3},{5,4},{6,5},{7,6},{9,8},{10,9},{11,10},{12... | collective-permute-start | bytes 18440 | tf_op jit(solution)/shard_map/ppermute | solution.py:25
  61.9 12.4 %collective-permute-start.5 = (f32[12,128]{1,0:T(8,128)S(1)}, f32[12,128]{1,0:T(8,128)S(1)}, u32[]{:S(2)}, u32[]{:S(2)}) collective-permute-start(f32[12,128]{1,0:T(8,128)S(1)} %copy-done.5), channel_id=1, source_target_pairs={{8,0},{16,8},{24,16},{9,1},{17,9},{25,17},{10,2},{18,10},{26,18},{... | collective-permute-start | bytes 18440 | tf_op jit(solution)/shard_map/ppermute | solution.py:25
  154.6 12.3 %all-to-all-start.2 = ((bf16[8,8,128]{2,1,0:T(8,128)(2,1)}), bf16[8,8,128]{2,1,0:T(8,128)(2,1)S(1)}, u32[]{:S(2)}, u32[]{:S(2)}) async-start(bf16[8,8,128]{2,1,0:T(8,128)(2,1)} %fusion.1), calls=%async_computation.2 | async-start | bytes 32768 | tf_op jit(solution)/shard_map/all_to_all | solution.py:344

commit v2 on v1

--- a/solution.py
+++ b/solution.py
@@ -13,6 +13,10 @@
 H = 8
 SLOTS = 64
 CODE = 2 * SLOTS
+TX = ("tz", "tw")
+PLANE = ("ty", "tw")
+PARTS = 2
+PART_ROWS = SIDE // PARTS
 LANES = 128
 GROUPS = LANES // SIDE
 F32 = jnp.float32
@@ -20,7 +24,7 @@
 
 
 def shifted(value, axis, steps):
-    count = lax.axis_size(axis)
+    count = math.prod(lax.axis_size(name) for name in axis)
     first, last = (max(0, -steps), min(count, count - steps))
     return lax.ppermute(value, axis, [(source, source + steps) for source in range(first, last)])
 
@@ -159,7 +163,8 @@
     return 1.0 + 3.0 * nearest / OV
 
 
-def pieces_kernel(shift_ref, pos_ref, tile_ref, tb_ref, side_ref, corner_ref, send_ref, work_ref):
+def pieces_kernel(shift_ref, pos_ref, tile_ref, tb_ref, side_ref, corner_ref, *rest):
+    send_refs, work_ref = rest[:PARTS], rest[PARTS]
     depth, length, _ = tile_ref.shape
 
     def edge_column(shape, dim):
@@ -178,7 +183,8 @@
         along_side = (mm_t(ry, side_ref[z]) + mm_t(ry_edge, corner_ref[z])).astype(BF16)
         resampled = mm(along, rx) + mm(along_side, rx_edge)
         work_ref[z] = weights * resampled
-    send_ref[...] = jnp.zeros_like(send_ref)
+    for send_ref in send_refs:
+        send_ref[...] = jnp.zeros_like(send_ref)
     grid_side = length // SIDE
 
     def row(py, carry):
@@ -186,7 +192,9 @@
         for q in range(length // LANES):
             parts = [work_ref[z, pl.ds(start, SIDE), q * LANES : (q + 1) * LANES] for z in range(depth)]
             for g, piece in enumerate(swap_groups(parts)):
-                send_ref[pos_ref[py * grid_side + q * GROUPS + g]] = piece.astype(BF16)
+                at = pos_ref[py * grid_side + q * GROUPS + g]
+                for c, send_ref in enumerate(send_refs):
+                    send_ref[at] = piece[c * PART_ROWS : (c + 1) * PART_ROWS].astype(BF16)
         return carry
 
     lax.fori_loop(0, grid_side, row, 0)
@@ -197,9 +205,9 @@
     smem = pl.BlockSpec(memory_space=pltpu.SMEM)
     return pl.pallas_call(
         pieces_kernel,
-        out_shape=jax.ShapeDtypeStruct((rows, SIDE, LANES), BF16),
+        out_shape=[jax.ShapeDtypeStruct((rows, PART_ROWS, LANES), BF16)] * PARTS,
         in_specs=[smem, smem, vmem, vmem, vmem, vmem],
-        out_specs=vmem,
+        out_specs=[vmem] * PARTS,
         scratch_shapes=[pltpu.VMEM(tile.shape, F32)],
         name="pieces",
         compiler_params=pltpu.CompilerParams(vmem_limit_bytes=40 * 2**20),
@@ -207,7 +215,8 @@
     )(shifts, position, tile, tb, side, corner)
 
 
-def join_kernel(slot_ref, got_ref, denom_ref, joined_ref, quads_ref, acc_ref, sum_ref, mean_ref):
+def gather_kernel(slot_ref, got_ref, *rest):
+    sum_refs, acc_ref = rest[:-1], rest[-1]
     acc_ref[...] = jnp.zeros_like(acc_ref)
     step = 8
 
@@ -218,6 +227,28 @@
         return carry
 
     lax.fori_loop(0, got_ref.shape[0] // step, add, 0)
+    for z, sum_ref in enumerate(sum_refs):
+        sum_ref[...] = acc_ref[pl.ds(z * SLOTS, SLOTS)].astype(BF16)
+
+
+def gather(slots, got, count):
+    vmem = pl.BlockSpec(memory_space=pltpu.VMEM)
+    smem = pl.BlockSpec(memory_space=pltpu.SMEM)
+    return pl.pallas_call(
+        gather_kernel,
+        out_shape=[jax.ShapeDtypeStruct((SLOTS,) + got.shape[1:], BF16)] * count,
+        in_specs=[smem, vmem],
+        out_specs=[vmem] * count,
+        scratch_shapes=[pltpu.VMEM((count * SLOTS + 1,) + got.shape[1:], F32)],
+        name="gather",
+        compiler_params=pltpu.CompilerParams(vmem_limit_bytes=24 * 2**20),
+        cost_estimate=pl.CostEstimate(flops=10**7, bytes_accessed=2**22, transcendentals=0),
+    )(slots, got)
+
+
+def join_kernel(*refs):
+    got_refs, (denom_ref, joined_ref, quads_ref, sum_ref, mean_ref) = refs[:-5], refs[-5:]
+    count = len(got_refs) // PARTS
     row = iota((LANES, LANES), 0)
     column = iota((LANES, LANES), 1)
     half = SIDE // 2
@@ -227,7 +258,14 @@
     rows = batch * SIDE
     for c in range(SLOTS // batch):
         part = pl.ds(c * batch, batch)
-        value = (acc_ref[part] / jnp.maximum(denom_ref[part], 1.0)).astype(BF16).reshape(rows, LANES)
+        numer = []
+        for p in range(PARTS):
+            total = got_refs[p * count][part].astype(F32)
+            for z in range(1, count):
+                total += got_refs[p * count + z][part].astype(F32)
+            numer.append(total)
+        numer = jnp.concatenate(numer, axis=1)
+        value = (numer / jnp.maximum(denom_ref[part], 1.0)).astype(BF16).reshape(rows, LANES)
         mean_ref[...] = value.astype(F32)
         sum_ref[...] = mm(value, pool_one)
         level = (sum_ref[pl.ds(0, rows // 2, stride=2), :] + sum_ref[pl.ds(1, rows // 2, stride=2), :]) * 0.125
@@ -241,7 +279,7 @@
             joined_ref[part, pl.ds(g * high, high), :] = piece.reshape(batch, high, LANES).astype(BF16)
 
 
-def join(slots, got, denom):
+def join(got, denom):
     vmem = pl.BlockSpec(memory_space=pltpu.VMEM)
     smem = pl.BlockSpec(memory_space=pltpu.SMEM)
     return pl.pallas_call(
@@ -250,17 +288,16 @@
             jax.ShapeDtypeStruct((SLOTS, SIDE, LANES), BF16),
             jax.ShapeDtypeStruct((SLOTS * SIDE // 4, LANES), F32),
         ],
-        in_specs=[smem, vmem, vmem],
+        in_specs=[vmem] * (len(got) + 1),
         out_specs=[vmem, vmem],
         scratch_shapes=[
-            pltpu.VMEM((SLOTS + 1, SIDE, LANES), F32),
             pltpu.VMEM((SLOTS // 4 * SIDE, LANES), F32),
             pltpu.VMEM((SLOTS // 4 * SIDE, LANES), F32),
         ],
         name="join",
         compiler_params=pltpu.CompilerParams(vmem_limit_bytes=32 * 2**20),
         cost_estimate=pl.CostEstimate(flops=10**8, bytes_accessed=2**23, transcendentals=0),
-    )(slots, got, denom)
+    )(*got, denom)
 
 
 def assemble(quadrant_blocks):
@@ -282,7 +319,9 @@
 def per_device(tiles, shifts, piece_target, coarse_target):
     tile = tiles[0, 0]
     count_y = lax.axis_size("ty")
-    count_x = lax.axis_size("tx")
+    count_z = lax.axis_size("tz")
+    count_w = lax.axis_size("tw")
+    count_x = count_z * count_w
     devices = count_y * count_x
     depth, length, _ = tile.shape
     pieces_n = (length // SIDE) ** 2
@@ -292,38 +331,56 @@
     owners = targets // SLOTS
     order = jnp.arange(pieces_n, dtype=jnp.int32)
     earlier = (owners[:, None] == owners[None, :]) & (order[None, :] < order[:, None])
-    position = owners * capacity + jnp.sum(earlier.astype(jnp.int32), axis=1)
+    owner_y, owner_x = owners // count_x, owners % count_x
+    owner_z, owner_w = owner_x // count_w, owner_x % count_w
+    place = (owner_y * count_w + owner_w) * count_z + owner_z
+    position = place * capacity + jnp.sum(earlier.astype(jnp.int32), axis=1)
     codes = order * CODE + targets % SLOTS - SLOTS
     rows = jnp.arange(devices * capacity, dtype=jnp.int32)
     send_codes = SLOTS + jnp.sum(
         jnp.where(position[None, :] == rows[:, None], codes[None, :], 0), axis=1
     )
-    got_codes = lax.all_to_all(send_codes, ("ty", "tx"), split_axis=0, concat_axis=0, tiled=True)
-
-    top = shifted(tile[:, length - H :, :], "ty", 1)
-    bottom = shifted(tile[:, :H, :], "ty", -1)
+    got_codes = lax.all_to_all(send_codes, PLANE, split_axis=0, concat_axis=0, tiled=True)
+
+    top = shifted(tile[:, length - H :, :], ("ty",), 1)
+    bottom = shifted(tile[:, :H, :], ("ty",), -1)
     tb = jnp.concatenate([top, bottom], axis=1)
     last = jnp.concatenate([tile[:, :, length - H :], tb[:, :, length - H :]], axis=1)
     first = jnp.concatenate([tile[:, :, :H], tb[:, :, :H]], axis=1)
-    left = shifted(last.transpose(0, 2, 1), "tx", 1)
-    right = shifted(first.transpose(0, 2, 1), "tx", -1)
+    left = shifted(last.transpose(0, 2, 1), TX, 1)
+    right = shifted(first.transpose(0, 2, 1), TX, -1)
     side = jnp.concatenate([left, right], axis=1)
     right_bins, left_bins, bottom_bins, top_bins = all_bins(tile)
     position, got_codes, left_bins, top_bins = lax.optimization_barrier(
         (position, got_codes, left_bins, top_bins)
     )
-    next_left = shifted(left_bins, "tx", -1)
-    next_top = shifted(top_bins, "ty", -1)
+    next_left = shifted(left_bins, TX, -1)
+    next_top = shifted(top_bins, ("ty",), -1)
     send = make_pieces(
         shifts[0, 0], position, tile, tb, side[:, :, :length], side[:, :, length:], devices * capacity
     )
-    got = lax.all_to_all(send, ("ty", "tx"), split_axis=0, concat_axis=0, tiled=True)
+    got = [lax.all_to_all(part, PLANE, split_axis=0, concat_axis=0, tiled=True) for part in send]
+
+    me_z = lax.axis_index("tz")
+    slots = got_codes % CODE
+    turn = (rows // capacity - me_z) % count_z
+    dense = count_z * SLOTS
+    slots = jnp.where(slots < SLOTS, turn * SLOTS + slots, dense)
+
+    def turned(values):
+        ring = range(count_z)
+        return [values[0]] + [
+            lax.ppermute(values[r], "tz", [(z, (z + r) % count_z) for z in ring]) for r in ring[1:]
+        ]
+
+    sums = [value for part in got for value in turned(gather(slots, part, count_z))]
 
     corr_right, corr_below = phase_surfaces(right_bins, next_left, bottom_bins, next_top)
-    slots = got_codes % CODE
-    slot_marks = slots[None, :] == jnp.arange(SLOTS, dtype=jnp.int32)[:, None]
+    slot_marks = slots[None, :] == jnp.arange(dense, dtype=jnp.int32)[:, None]
     place_marks = (got_codes // CODE)[:, None] == order[None, :]
     counts = mm(slot_marks.astype(BF16), place_marks.astype(BF16)).astype(BF16)
+    counts = turned(list(counts.reshape(count_z, SLOTS, -1)))
+    counts = sum(value.astype(F32) for value in counts).astype(BF16)
     denom = mm(counts, patch_weights(length, depth)).reshape(SLOTS, SIDE, LANES)
 
     coarse_ids = coarse_target[0, 0]
@@ -334,14 +391,14 @@
     coarse_pos = owner * per_peer + jnp.sum(ahead.astype(jnp.int32), axis=1)
     ordering = (coarse_pos[None, :] == number[:, None]).astype(BF16)
     locals_ = jnp.broadcast_to((coarse_ids % SLOTS).astype(BF16)[:, None], (SLOTS, SLOTS))
-    got, denom, slots, ordering, locals_, corr_right, corr_below = lax.optimization_barrier(
-        (got, denom, slots, ordering, locals_, corr_right, corr_below)
-    )
-    joined, quads = join(slots, got, denom)
+    sums, denom, ordering, locals_, corr_right, corr_below = lax.optimization_barrier(
+        (sums, denom, ordering, locals_, corr_right, corr_below)
+    )
+    joined, quads = join(sums, denom)
     joined = joined.reshape(SLOTS, depth * SIDE * SIDE)
     flat = quads[:, : SIDE // 4].astype(BF16).reshape(SLOTS, -1)
     send_quads = mm(ordering, jnp.concatenate([flat, locals_], axis=1)).astype(BF16)
-    got_quads = lax.all_to_all(send_quads, "tx", split_axis=0, concat_axis=0, tiled=True)
+    got_quads = lax.all_to_all(send_quads, TX, split_axis=0, concat_axis=0, tiled=True)
     width = flat.shape[1]
     got_local = got_quads[:, width].astype(jnp.int32)
     place = (got_local[None, :] == number[:, None]).astype(BF16)
@@ -351,16 +408,17 @@
 
 
 def solution(mesh):
-    placed = (
-        P("ty", "tx", None, None, None),
-        P("ty", "tx", None),
-        P("ty", "tx", None),
-        P("ty", "tx", None),
-    )
+    count_y, count_x = mesh.devices.shape
+    count_z = math.gcd(count_x, 4)
+    split = jax.sharding.Mesh(
+        mesh.devices.reshape(count_y, count_z, count_x // count_z), ("ty", "tz", "tw")
+    )
+    placed = (P("ty", TX, None, None, None), P("ty", TX, None), P("ty", TX, None), P("ty", TX, None))
+    every = ("ty",) + TX
     return jax.shard_map(
         per_device,
-        mesh=mesh,
+        mesh=split,
         in_specs=placed,
-        out_specs=(P(("ty", "tx"), None), P(("ty", "tx"), None), P("ty", "tx"), P("ty", "tx")),
+        out_specs=(P(every, None), P(every, None), P("ty", TX), P("ty", TX)),
         check_vma=False,
     )

time: 169 us -> 182 us (1.077)
  starting transfers between devices: 36.6 us -> 54.9 us
  waiting for transfers between devices: 82.7 us -> 69.8 us
  local copies, waits for them, and re-layouts: 20.8 us -> 24.1 us
  Pallas kernels: 20.5 us -> 22.7 us
    all_to_all x3 -> x4, waiting for transfers between devices: 73.4 us -> 31.2 us  [the longest x2 25.7 us: per_device(): lax.all_to_all(part, PLANE, split_axis=0, concat_axis=0, tiled=True)]
    ppermute x0 -> x9, waiting for transfers between devices: none -> 25.3 us  [turned(): lax.ppermute(values[r], 'tz', [(z, (z + r) % count_z) for z in ring])]
    ppermute x0 -> x9, starting transfers between devices: none -> 16.4 us  [turned(): lax.ppermute(values[r], 'tz', [(z, (z + r) % count_z) for z in ring])]
    pallas_call x1 -> x3, Pallas kernels: 7.16 us -> 14.4 us  [the longest x2 7.25 us: gather(): pl.pallas_call(gather_kernel, out_shape=[jax.ShapeDtypeStruct((SLOTS,) +...]
    pallas_call x1, Pallas kernels: 6.25 us -> 1.1 us  [join(): pl.pallas_call(join_kernel, out_shape=[jax.ShapeDtypeStruct((SLOTS, SIDE,...]
    ppermute x6, waiting for transfers between devices: 9.34 us -> 13.2 us  [shifted(): lax.ppermute(value, axis, [(source, source + steps) for source in range(f...]
    unnamed x21 -> x31, local copies, waits for them, and re-layouts: 8.82 us -> 10.9 us
    all_to_all x3 -> x4, starting transfers between devices: 24.5 us -> 26.2 us  [the longest x2 12.2 us: per_device(): lax.all_to_all(part, PLANE, split_axis=0, concat_axis=0, tiled=True)]
  transfers between devices with their start and end apart: 9 -> 19, of which waited for: 3 -> 7; matrix products, arithmetic and copies ran while one was open for 12% -> 13% of each run, Pallas kernels for 4% -> 8%
where the time goes in v2:
time: 182 us; the launch traced here: 181 us
  waiting for transfers between devices  69.8 us (38%)
  starting transfers between devices  54.9 us (30%)
  local copies, waits for them, and re-layouts  24.1 us (13%)
  Pallas kernels  22.7 us (12%)
  other arithmetic  5.46 us (3%)
  matrix products  2.82 us (2%)
    all_to_all x2, waiting for transfers between devices, per_device(): lax.all_to_all(part, PLANE, split_axis=0, concat_axis=0, tiled=True)  25.7 us
    ppermute x9, waiting for transfers between devices, turned(): lax.ppermute(values[r], 'tz', [(z, (z + r) % count_z) for z in ring])  25.3 us
    ppermute x9, starting transfers between devices, turned(): lax.ppermute(values[r], 'tz', [(z, (z + r) % count_z) for z in ring])  16.4 us
    ppermute x6, waiting for transfers between devices, shifted(): lax.ppermute(value, axis, [(source, source + steps) for source in range(f...  13.2 us
    ppermute x6, starting transfers between devices, shifted(): lax.ppermute(value, axis, [(source, source + steps) for source in range(f...  12.3 us
    all_to_all x2, starting transfers between devices, per_device(): lax.all_to_all(part, PLANE, split_axis=0, concat_axis=0, tiled=True)  12.2 us
    unnamed x31, local copies, waits for them, and re-layouts  10.9 us
    all_to_all x1, starting transfers between devices, per_device(): lax.all_to_all(send_quads, TX, split_axis=0, concat_axis=0, tiled=True)  8.79 us
  transfers between devices with their start and end apart: 19, of which 7 were waited for; matrix products, arithmetic and copies ran while one was open for 13% of the time, Pallas kernels for 8%

profile of v2, /device:TPU:0, one launch (start us, length us, event | category | flops | bytes accessed | tf_op | source)
XLA Modules:
  0.0 180.7 jit_solution(10772666745517306316)
XLA Ops:
  0.6 0.7 fusion.40
  1.3 0.2 convert_reduce_fusion
  1.7 0.7 add.223
  2.4 5.2 %all-to-all-start = ((s32[8,64,1]{1,2,0:T(1,128)}), s32[8,64,1]{1,2,0:T(1,128)S(1)}, u32[]{:S(2)}, u32[]{:S(2)}) async-start(s32[8,64,1]{1,2,0:T(1,128)} %bitcast.1), calls=%async_computation | async-start | bytes 8192 | tf_op jit(solution)/shard_map/all_to_all | solution.py:343
  7.5 2.8 %copy.44 = bf16[1,1,4,512,512]{3,4,2,1,0:T(8,128)(2,1)S(1)} copy(bf16[1,1,4,512,512]{4,3,2,1,0:T(8,128)(2,1)} %param.4) | data formatting | bytes 4194304 | tf_op args[0]
  10.3 1.2 fusion.44
  11.5 1.3 collective-permute-start.1
  12.8 3.1 %collective-permute-start = (bf16[4,8,512]{1,2,0:T(8,128)(2,1)}, bf16[4,8,512]{1,2,0:T(8,128)(2,1)S(1)}, u32[]{:S(2)}, u32[]{:S(2)}) collective-permute-start(bf16[4,8,512]{1,2,0:T(8,128)(2,1)} %get-tuple-element.92), channel_id=1, source_target_pairs={{0,8},{8,16},{16,24},{1,9},{9,17},{17,25},{2,10},{10,18},{18,26},{... | collective-permute-start | bytes 98312 | tf_op jit(solution)/shard_map/ppermute | solution.py:29
  15.9 3.2 %bins.1 = (f32[12,128]{1,0:T(8,128)}, f32[12,128]{1,0:T(8,128)}, f32[12,128]{1,0:T(8,128)}, f32[12,128]{1,0:T(8,128)}) custom-call(bf16[4,512,512]{2,1,0:T(8,128)(2,1)} %bitcast.51), custom_call_target="tpu_custom_call" | custom-call | flops 100000000 | bytes 2097152 | tf_op jit(solution)/shard_map/bins/pallas_call | solution.py:72
  19.1 0.5 broadcast.563
  19.6 0.7 reduce.5
  20.5 3.9 %collective-permute-start.2 = (bf16[4,8,528]{2,1,0:T(8,128)(2,1)S(1)}, bf16[4,8,528]{2,1,0:T(8,128)(2,1)S(1)}, u32[]{:S(2)}, u32[]{:S(2)}) collective-permute-start(bf16[4,8,528]{2,1,0:T(8,128)(2,1)S(1)} %maximum_bitcast_fusion), channel_id=1, source_target_pairs={{0,1},{1,2},{2,3},{3,4},{4,5},{5,6},{6,7},{8,9},{9,10},{10,11},{11... | collective-permute-start | bytes 101384 | tf_op jit(solution)/shard_map/ppermute | solution.py:29
  24.5 1.1 pad_maximum_fusion
  25.6 1.2 copy.47.tb_ref
  26.8 1.3 collective-permute-start.3
  28.1 4.6 %collective-permute-done.3 = bf16[4,8,528]{2,1,0:T(8,128)(2,1)S(1)} collective-permute-done((bf16[4,8,528]{2,1,0:T(8,128)(2,1)S(1)}, bf16[4,8,528]{2,1,0:T(8,128)(2,1)S(1)}, u32[]{:S(2)}, u32[]{:S(2)}) %collective-permute-start.3) | collective-permute-done | bytes 33824 | tf_op jit(solution)/shard_map/ppermute | solution.py:29
  32.7 7.2 %pieces.1 = (bf16[512,16,128]{2,1,0:T(8,128)(2,1)S(1)}, bf16[512,16,128]{2,1,0:T(8,128)(2,1)S(1)}) custom-call(s32[2]{0:T(128)S(1)} %bitcast.54, s32[256]{0:T(256)S(1)} %multiply_add_fusion.1.pos_ref, bf16[4,512,512]{2,1,0:T(8,128)(2,1)S(1)} %bitcast.52, bf16[4,16,512]{2,1,0:T(8,128)(2,1)S(1)} %copy.47.tb_ref, bf16[4,16,512]{2,1,0:T(8,128)(2,1)S(1)} %slice.65.side_ref, ...), custom_call_target="tpu_custom_call" | custom-call | flops 2000000000 | bytes 8388608 | tf_op jit(solution)/shard_map/pieces/pallas_call | solution.py:206
  39.9 1.3 copy-done.3
  41.2 1.3 copy-done.4
  42.5 8.6 %all-to-all-start.1 = ((bf16[512,16,128]{2,1,0:T(8,128)(2,1)}), bf16[512,16,128]{2,1,0:T(8,128)(2,1)S(1)}, u32[]{:S(2)}, u32[]{:S(2)}) async-start(bf16[512,16,128]{2,1,0:T(8,128)(2,1)} %copy-done.4), calls=%async_computation.1 | async-start | bytes 4194304 | tf_op jit(solution)/shard_map/all_to_all | solution.py:362
  51.3 25.7 %all-to-all-done.1.got_ref = bf16[512,16,128]{2,1,0:T(8,128)(2,1)S(1)} async-done(((bf16[512,16,128]{2,1,0:T(8,128)(2,1)}), bf16[512,16,128]{2,1,0:T(8,128)(2,1)S(1)}, u32[]{:S(2)}, u32[]{:S(2)}) %all-to-all-start.1) | async-done | bytes 2097184 | tf_op jit(solution)/shard_map/all_to_all | solution.py:362
  76.9 1.3 copy-done.1
  78.3 3.6 %all-to-all-start.2 = ((bf16[512,16,128]{2,1,0:T(8,128)(2,1)}), bf16[512,16,128]{2,1,0:T(8,128)(2,1)S(1)}, u32[]{:S(2)}, u32[]{:S(2)}) async-start(bf16[512,16,128]{2,1,0:T(8,128)(2,1)} %copy-done.3), calls=%async_computation.2 | async-start | bytes 4194304 | tf_op jit(solution)/shard_map/all_to_all | solution.py:362
  82.0 0.2 convert_reduce_fusion.2
  82.2 0.9 sine_multiply_fusion
  83.1 0.6 fusion.15
  83.7 0.4 multiply_convert_fusion
  84.1 1.3 collective-permute-start.13
  85.5 0.4 convolution_convert_fusion
  85.8 3.9 %gather.2 = (bf16[64,16,128]{2,1,0:T(8,128)(2,1)S(1)}, bf16[64,16,128]{2,1,0:T(8,128)(2,1)}, bf16[64,16,128]{2,1,0:T(8,128)(2,1)S(1)}, bf16[64,16,128]{2,1,0:T(8,128)(2,1)S(1)}) custom-call(s32[512]{0:T(512)S(1)} %get-tuple-element.100.slot_ref, bf16[512,16,128]{2,1,0:T(8,128)(2,1)S(1)} %copy-done.2), custom_call_target="tpu_custom_call" | custom-call | flops 10000000 | bytes 4194304 | tf_op jit(solution)/shard_map/gather/pallas_call | solution.py:237
  89.8 3.9 %collective-permute-start.4 = (bf16[64,16,128]{2,1,0:T(8,128)(2,1)}, bf16[64,16,128]{2,1,0:T(8,128)(2,1)S(1)}, u32[]{:S(2)}, u32[]{:S(2)}) collective-permute-start(bf16[64,16,128]{2,1,0:T(8,128)(2,1)} %get-tuple-element.45), channel_id=1, source_target_pairs={{0,2},{2,4},{4,6},{6,0},{1,3},{3,5},{5,7},{7,1},{8,10},{10,12},{12... | collective-permute-start | bytes 786440 | tf_op jit(solution)/shard_map/ppermute | solution.py:373
  93.7 0.6 fusion.45
  94.3 2.1 %collective-permute-start.12 = (bf16[64,256]{1,0:T(8,128)(2,1)}, bf16[64,256]{1,0:T(8,128)(2,1)}, u32[]{:S(2)}, u32[]{:S(2)}) collective-permute-start(bf16[64,256]{1,0:T(8,128)(2,1)} %get-tuple-element.97), channel_id=1, source_target_pairs={{0,6},{2,0},{4,2},{6,4},{1,7},{3,1},{5,3},{7,5},{8,14},{10,8},{12,... | collective-permute-start | bytes 98312 | tf_op jit(solution)/shard_map/ppermute | solution.py:373
  96.4 1.0 collective-permute-start.11
  97.4 1.6 collective-permute-start.10
  99.0 8.7 %collective-permute-done.13 = f32[12,128]{1,0:T(8,128)S(1)} collective-permute-done((f32[12,128]{1,0:T(8,128)S(1)}, f32[12,128]{1,0:T(8,128)S(1)}, u32[]{:S(2)}, u32[]{:S(2)}) %collective-permute-start.13) | collective-permute-done | bytes 6176 | tf_op jit(solution)/shard_map/ppermute | solution.py:29
  107.7 1.5 collective-permute-start.14
  109.2 2.4 %copy.59 = bf16[32,8,32,128]{3,1,2,0:T(8,128)(2,1)} copy(bf16[32,8,32,128]{3,2,1,0:T(8,128)(2,1)S(1)} %bitcast.56) | data formatting | bytes 4194304
  111.6 4.1 %copy.54 = bf16[4096,256]{1,0:T(8,128)(2,1)} copy(bf16[4096,256]{0,1:T(8,128)(2,1)} %bitcast.57) | data formatting | bytes 4194304 | tf_op jit(solution)/shard_map/dot_general | solution.py:41
  115.7 0.6 pad.20.ca_ref
  116.3 0.6 pad.21.sa_ref
  116.9 0.6 pad.22.r_ref
  117.5 0.6 pad.24.b_ref
  118.1 0.6 pad.23.l_ref
  118.7 0.6 pad.25.t_ref
  119.3 3.9 %phase.1 = (f32[16,128]{1,0:T(8,128)}, f32[16,128]{1,0:T(8,128)}) custom-call(f32[16,16]{1,0:T(8,128)} %pad.20.ca_ref, f32[16,16]{1,0:T(8,128)} %pad.21.sa_ref, f32[128,128]{1,0:T(8,128)} %get-tuple-element.106.cb_ref, f32[128,128]{1,0:T(8,128)} %get-tuple-element.105.sb_ref, f32[16,128]{1,0:T(8,128)} %pad.22.r_ref, f32[16,128]{1,0:T(8,128)} %pad.23.l_ref, ...), custom_call_target="tpu_custom_call" | custom-call | flops 100000000 | bytes 262144 | tf_op jit(solution)/shard_map/phase/pallas_call | solution.py:120
  123.2 2.6 %collective-permute-start.5 = (bf16[64,16,128]{2,1,0:T(8,128)(2,1)S(1)}, bf16[64,16,128]{2,1,0:T(8,128)(2,1)S(1)}, u32[]{:S(2)}, u32[]{:S(2)}) collective-permute-start(bf16[64,16,128]{2,1,0:T(8,128)(2,1)S(1)} %get-tuple-element.46), channel_id=1, source_target_pairs={{0,4},{2,6},{4,0},{6,2},{1,5},{3,7},{5,1},{7,3},{8,12},{10,14},{12... | collective-permute-start | bytes 786440 | tf_op jit(solution)/shard_map/ppermute | solution.py:373
  125.8 3.3 %gather.3 = (bf16[64,16,128]{2,1,0:T(8,128)(2,1)S(1)}, bf16[64,16,128]{2,1,0:T(8,128)(2,1)S(1)}, bf16[64,16,128]{2,1,0:T(8,128)(2,1)S(1)}, bf16[64,16,128]{2,1,0:T(8,128)(2,1)S(1)}) custom-call(s32[512]{0:T(512)S(1)} %get-tuple-element.100.slot_ref, bf16[512,16,128]{2,1,0:T(8,128)(2,1)S(1)} %all-to-all-done.2.got_ref), custom_call_target="tpu_custom_call" | custom-call | flops 10000000 | bytes 4194304 | tf_op jit(solution)/shard_map/gather/pallas_call | solution.py:237
  129.1 1.4 collective-permute-start.6
  130.5 0.7 collective-permute-start.7
  131.2 0.3 collective-permute-start.8
  131.5 2.9 %collective-permute-start.9 = (bf16[64,16,128]{2,1,0:T(8,128)(2,1)S(1)}, bf16[64,16,128]{2,1,0:T(8,128)(2,1)S(1)}, u32[]{:S(2)}, u32[]{:S(2)}) collective-permute-start(bf16[64,16,128]{2,1,0:T(8,128)(2,1)S(1)} %get-tuple-element.52), channel_id=1, source_target_pairs={{0,6},{2,0},{4,2},{6,4},{1,7},{3,1},{5,3},{7,5},{8,14},{10,8},{12,... | collective-permute-start | bytes 786440 | tf_op jit(solution)/shard_map/ppermute | solution.py:373
  134.4 1.5 fusion.11
  135.9 2.9 %collective-permute-done.5.refs_2_ = bf16[64,16,128]{2,1,0:T(8,128)(2,1)S(1)} collective-permute-done((bf16[64,16,128]{2,1,0:T(8,128)(2,1)S(1)}, bf16[64,16,128]{2,1,0:T(8,128)(2,1)S(1)}, u32[]{:S(2)}, u32[]{:S(2)}) %collective-permute-start.5) | collective-permute-done | bytes 262176 | tf_op jit(solution)/shard_map/ppermute | solution.py:373
  138.8 9.6 %collective-permute-done.6.refs_3_ = bf16[64,16,128]{2,1,0:T(8,128)(2,1)S(1)} collective-permute-done((bf16[64,16,128]{2,1,0:T(8,128)(2,1)S(1)}, bf16[64,16,128]{2,1,0:T(8,128)(2,1)S(1)}, u32[]{:S(2)}, u32[]{:S(2)}) %collective-permute-start.6) | collective-permute-done | bytes 262176 | tf_op jit(solution)/shard_map/ppermute | solution.py:373
  148.4 12.9 %collective-permute-done.8.refs_6_ = bf16[64,16,128]{2,1,0:T(8,128)(2,1)S(1)} collective-permute-done((bf16[64,16,128]{2,1,0:T(8,128)(2,1)S(1)}, bf16[64,16,128]{2,1,0:T(8,128)(2,1)S(1)}, u32[]{:S(2)}, u32[]{:S(2)}) %collective-permute-start.8) | collective-permute-done | bytes 262176 | tf_op jit(solution)/shard_map/ppermute | solution.py:373
  161.3 0.6 copy.49.refs_8_
  162.0 1.1 join.1
  163.2 0.8 fusion
  164.0 8.8 %all-to-all-start.3 = ((bf16[8,8,128]{2,1,0:T(8,128)(2,1)}), bf16[8,8,128]{2,1,0:T(8,128)(2,1)S(1)}, u32[]{:S(2)}, u32[]{:S(2)}) async-start(bf16[8,8,128]{2,1,0:T(8,128)(2,1)} %fusion), calls=%async_computation.3 | async-start | bytes 32768 | tf_op jit(solution)/shard_map/all_to_all | solution.py:401
  172.8 1.0 copy.60
  173.8 5.6 %all-to-all-done.3 = bf16[8,8,128]{2,1,0:T(8,128)(2,1)S(1)} async-done(((bf16[8,8,128]{2,1,0:T(8,128)(2,1)}), bf16[8,8,128]{2,1,0:T(8,128)(2,1)S(1)}, u32[]{:S(2)}, u32[]{:S(2)}) %all-to-all-start.3) | async-done | bytes 16416 | tf_op jit(solution)/shard_map/all_to_all | solution.py:401
  179.9 0.2 copy.50
  180.1 0.7 copy.51
  (61 shorter events, 1.4 us)
Async XLA Ops:
  2.4 16.8 %all-to-all-start = ((s32[8,64,1]{1,2,0:T(1,128)}), s32[8,64,1]{1,2,0:T(1,128)S(1)}, u32[]{:S(2)}, u32[]{:S(2)}) async-start(s32[8,64,1]{1,2,0:T(1,128)} %bitcast.1), calls=%async_computation | async-start | bytes 8192 | tf_op jit(solution)/shard_map/all_to_all | solution.py:343
  11.5 8.9 %collective-permute-start.1 = (bf16[4,8,512]{1,2,0:T(8,128)(2,1)}, bf16[4,8,512]{1,2,0:T(8,128)(2,1)S(1)}, u32[]{:S(2)}, u32[]{:S(2)}) collective-permute-start(bf16[4,8,512]{1,2,0:T(8,128)(2,1)} %get-tuple-element.93), channel_id=1, source_target_pairs={{8,0},{16,8},{24,16},{9,1},{17,9},{25,17},{10,2},{18,10},{26,18},{... | collective-permute-start | bytes 98312 | tf_op jit(solution)/shard_map/ppermute | solution.py:29
  12.8 7.6 %collective-permute-start = (bf16[4,8,512]{1,2,0:T(8,128)(2,1)}, bf16[4,8,512]{1,2,0:T(8,128)(2,1)S(1)}, u32[]{:S(2)}, u32[]{:S(2)}) collective-permute-start(bf16[4,8,512]{1,2,0:T(8,128)(2,1)} %get-tuple-element.92), channel_id=1, source_target_pairs={{0,8},{8,16},{16,24},{1,9},{9,17},{17,25},{2,10},{10,18},{18,26},{... | collective-permute-start | bytes 98312 | tf_op jit(solution)/shard_map/ppermute | solution.py:29
  19.1 13.6 %copy-start = (bf16[1,1,4,512,512]{4,3,2,1,0:T(8,128)(2,1)S(1)}, bf16[1,1,4,512,512]{4,3,2,1,0:T(8,128)(2,1)}, u32[]{:S(2)}) copy-start(bf16[1,1,4,512,512]{4,3,2,1,0:T(8,128)(2,1)} %param.4) | copy-start | bytes 6291460
  19.1 13.6 %copy-start.5 = (s32[1,1,2]{2,1,0:T(1,128)S(1)}, s32[1,1,2]{2,1,0:T(1,128)}, u32[]{:S(2)}) copy-start(s32[1,1,2]{2,1,0:T(1,128)} %param.5) | copy-start | bytes 28
  20.5 7.5 %collective-permute-start.2 = (bf16[4,8,528]{2,1,0:T(8,128)(2,1)S(1)}, bf16[4,8,528]{2,1,0:T(8,128)(2,1)S(1)}, u32[]{:S(2)}, u32[]{:S(2)}) collective-permute-start(bf16[4,8,528]{2,1,0:T(8,128)(2,1)S(1)} %maximum_bitcast_fusion), channel_id=1, source_target_pairs={{0,1},{1,2},{2,3},{3,4},{4,5},{5,6},{6,7},{8,9},{9,10},{10,11},{11... | collective-permute-start | bytes 101384 | tf_op jit(solution)/shard_map/ppermute | solution.py:29
  26.8 5.9 %collective-permute-start.3 = (bf16[4,8,528]{2,1,0:T(8,128)(2,1)S(1)}, bf16[4,8,528]{2,1,0:T(8,128)(2,1)S(1)}, u32[]{:S(2)}, u32[]{:S(2)}) collective-permute-start(bf16[4,8,528]{2,1,0:T(8,128)(2,1)S(1)} %maximum_bitcast_fusion.1), channel_id=1, source_target_pairs={{1,0},{2,1},{3,2},{4,3},{5,4},{6,5},{7,6},{9,8},{10,9},{11,10},{12... | collective-permute-start | bytes 101384 | tf_op jit(solution)/shard_map/ppermute | solution.py:29
  39.9 1.3 copy-start.3
  41.2 1.3 copy-start.4
  42.5 8.7 %copy-start.12 = (s32[1,1,64]{2,1,0:T(1,128)S(1)}, s32[1,1,64]{2,1,0:T(1,128)}, u32[]{:S(2)}) copy-start(s32[1,1,64]{2,1,0:T(1,128)} %param.7) | copy-start | bytes 772
  42.5 34.4 %all-to-all-start.1 = ((bf16[512,16,128]{2,1,0:T(8,128)(2,1)}), bf16[512,16,128]{2,1,0:T(8,128)(2,1)S(1)}, u32[]{:S(2)}, u32[]{:S(2)}) async-start(bf16[512,16,128]{2,1,0:T(8,128)(2,1)} %copy-done.4), calls=%async_computation.1 | async-start | bytes 4194304 | tf_op jit(solution)/shard_map/all_to_all | solution.py:362
  76.9 1.3 copy-start.1
  78.3 47.5 %all-to-all-start.2 = ((bf16[512,16,128]{2,1,0:T(8,128)(2,1)}), bf16[512,16,128]{2,1,0:T(8,128)(2,1)S(1)}, u32[]{:S(2)}, u32[]{:S(2)}) async-start(bf16[512,16,128]{2,1,0:T(8,128)(2,1)} %copy-done.3), calls=%async_computation.2 | async-start | bytes 4194304 | tf_op jit(solution)/shard_map/all_to_all | solution.py:362
  81.9 2.2 %copy-start.11 = (f32[12,128]{1,0:T(8,128)S(1)}, f32[12,128]{1,0:T(8,128)}, u32[]{:S(2)}) copy-start(f32[12,128]{1,0:T(8,128)} %get-tuple-element.54) | copy-start | bytes 18436
  81.9 3.9 %copy-start.2 = (bf16[512,16,128]{2,1,0:T(8,128)(2,1)S(1)}, bf16[512,16,128]{2,1,0:T(8,128)(2,1)}, u32[]{:S(2)}) copy-start(bf16[512,16,128]{2,1,0:T(8,128)(2,1)} %copy-done.1) | copy-start | bytes 6291460
  83.7 23.9 %copy-start.10 = (f32[12,128]{1,0:T(8,128)S(1)}, f32[12,128]{1,0:T(8,128)}, u32[]{:S(2)}) copy-start(f32[12,128]{1,0:T(8,128)} %get-tuple-element.56) | copy-start | bytes 18436
  84.1 23.5 %collective-permute-start.13 = (f32[12,128]{1,0:T(8,128)S(1)}, f32[12,128]{1,0:T(8,128)S(1)}, u32[]{:S(2)}, u32[]{:S(2)}) collective-permute-start(f32[12,128]{1,0:T(8,128)S(1)} %copy-done.11), channel_id=1, source_target_pairs={{1,0},{2,1},{3,2},{4,3},{5,4},{6,5},{7,6},{9,8},{10,9},{11,10},{12... | collective-permute-start | bytes 18440 | tf_op jit(solution)/shard_map/ppermute | solution.py:29
  89.8 41.7 %collective-permute-start.4 = (bf16[64,16,128]{2,1,0:T(8,128)(2,1)}, bf16[64,16,128]{2,1,0:T(8,128)(2,1)S(1)}, u32[]{:S(2)}, u32[]{:S(2)}) collective-permute-start(bf16[64,16,128]{2,1,0:T(8,128)(2,1)} %get-tuple-element.45), channel_id=1, source_target_pairs={{0,2},{2,4},{4,6},{6,0},{1,3},{3,5},{5,7},{7,1},{8,10},{10,12},{12... | collective-permute-start | bytes 786440 | tf_op jit(solution)/shard_map/ppermute | solution.py:373
  94.3 34.8 %collective-permute-start.12 = (bf16[64,256]{1,0:T(8,128)(2,1)}, bf16[64,256]{1,0:T(8,128)(2,1)}, u32[]{:S(2)}, u32[]{:S(2)}) collective-permute-start(bf16[64,256]{1,0:T(8,128)(2,1)} %get-tuple-element.97), channel_id=1, source_target_pairs={{0,6},{2,0},{4,2},{6,4},{1,7},{3,1},{5,3},{7,5},{8,14},{10,8},{12,... | collective-permute-start | bytes 98312 | tf_op jit(solution)/shard_map/ppermute | solution.py:373
  96.4 34.1 %collective-permute-start.11 = (bf16[64,256]{1,0:T(8,128)(2,1)}, bf16[64,256]{1,0:T(8,128)(2,1)}, u32[]{:S(2)}, u32[]{:S(2)}) collective-permute-start(bf16[64,256]{1,0:T(8,128)(2,1)} %get-tuple-element.98), channel_id=1, source_target_pairs={{0,4},{2,6},{4,0},{6,2},{1,5},{3,7},{5,1},{7,3},{8,12},{10,14},{12... | collective-permute-start | bytes 98312 | tf_op jit(solution)/shard_map/ppermute | solution.py:373
  97.4 33.8 %collective-permute-start.10 = (bf16[64,256]{1,0:T(8,128)(2,1)}, bf16[64,256]{1,0:T(8,128)(2,1)}, u32[]{:S(2)}, u32[]{:S(2)}) collective-permute-start(bf16[64,256]{1,0:T(8,128)(2,1)} %get-tuple-element.96), channel_id=1, source_target_pairs={{0,2},{2,4},{4,6},{6,0},{1,3},{3,5},{5,7},{7,1},{8,10},{10,12},{12... | collective-permute-start | bytes 98312 | tf_op jit(solution)/shard_map/ppermute | solution.py:373
  107.7 11.0 %collective-permute-start.14 = (f32[12,128]{1,0:T(8,128)S(1)}, f32[12,128]{1,0:T(8,128)S(1)}, u32[]{:S(2)}, u32[]{:S(2)}) collective-permute-start(f32[12,128]{1,0:T(8,128)S(1)} %copy-done.10), channel_id=1, source_target_pairs={{8,0},{16,8},{24,16},{9,1},{17,9},{25,17},{10,2},{18,10},{26,18},{... | collective-permute-start | bytes 18440 | tf_op jit(solution)/shard_map/ppermute | solution.py:29
  111.5 5.3 %copy-start.9 = (f32[12,128]{1,0:T(8,128)S(1)}, f32[12,128]{1,0:T(8,128)}, u32[]{:S(2)}) copy-start(f32[12,128]{1,0:T(8,128)} %get-tuple-element.53) | copy-start | bytes 18436
  111.6 5.9 %copy-start.8 = (f32[12,128]{1,0:T(8,128)S(1)}, f32[12,128]{1,0:T(8,128)}, u32[]{:S(2)}) copy-start(f32[12,128]{1,0:T(8,128)} %get-tuple-element.55) | copy-start | bytes 18436
  123.2 15.6 %collective-permute-start.5 = (bf16[64,16,128]{2,1,0:T(8,128)(2,1)S(1)}, bf16[64,16,128]{2,1,0:T(8,128)(2,1)S(1)}, u32[]{:S(2)}, u32[]{:S(2)}) collective-permute-start(bf16[64,16,128]{2,1,0:T(8,128)(2,1)S(1)} %get-tuple-element.46), channel_id=1, source_target_pairs={{0,4},{2,6},{4,0},{6,2},{1,5},{3,7},{5,1},{7,3},{8,12},{10,14},{12... | collective-permute-start | bytes 786440 | tf_op jit(solution)/shard_map/ppermute | solution.py:373
  125.8 8.6 %copy-start.6 = (bf16[4096,256]{1,0:T(8,128)(2,1)S(1)}, bf16[4096,256]{1,0:T(8,128)(2,1)}, u32[]{:S(2)}) copy-start(bf16[4096,256]{1,0:T(8,128)(2,1)} %copy.54) | copy-start | bytes 6291460
  129.1 19.3 %collective-permute-start.6 = (bf16[64,16,128]{2,1,0:T(8,128)(2,1)S(1)}, bf16[64,16,128]{2,1,0:T(8,128)(2,1)S(1)}, u32[]{:S(2)}, u32[]{:S(2)}) collective-permute-start(bf16[64,16,128]{2,1,0:T(8,128)(2,1)S(1)} %get-tuple-element.47), channel_id=1, source_target_pairs={{0,6},{2,0},{4,2},{6,4},{1,7},{3,1},{5,3},{7,5},{8,14},{10,8},{12,... | collective-permute-start | bytes 786440 | tf_op jit(solution)/shard_map/ppermute | solution.py:373
  130.5 17.9 %collective-permute-start.7 = (bf16[64,16,128]{2,1,0:T(8,128)(2,1)S(1)}, bf16[64,16,128]{2,1,0:T(8,128)(2,1)S(1)}, u32[]{:S(2)}, u32[]{:S(2)}) collective-permute-start(bf16[64,16,128]{2,1,0:T(8,128)(2,1)S(1)} %get-tuple-element.50), channel_id=1, source_target_pairs={{0,2},{2,4},{4,6},{6,0},{1,3},{3,5},{5,7},{7,1},{8,10},{10,12},{12... | collective-permute-start | bytes 786440 | tf_op jit(solution)/shard_map/ppermute | solution.py:373
  131.2 30.1 %collective-permute-start.8 = (bf16[64,16,128]{2,1,0:T(8,128)(2,1)S(1)}, bf16[64,16,128]{2,1,0:T(8,128)(2,1)S(1)}, u32[]{:S(2)}, u32[]{:S(2)}) collective-permute-start(bf16[64,16,128]{2,1,0:T(8,128)(2,1)S(1)} %get-tuple-element.51), channel_id=1, source_target_pairs={{0,4},{2,6},{4,0},{6,2},{1,5},{3,7},{5,1},{7,3},{8,12},{10,14},{12... | collective-permute-start | bytes 786440 | tf_op jit(solution)/shard_map/ppermute | solution.py:373
  131.5 29.8 %collective-permute-start.9 = (bf16[64,16,128]{2,1,0:T(8,128)(2,1)S(1)}, bf16[64,16,128]{2,1,0:T(8,128)(2,1)S(1)}, u32[]{:S(2)}, u32[]{:S(2)}) collective-permute-start(bf16[64,16,128]{2,1,0:T(8,128)(2,1)S(1)} %get-tuple-element.52), channel_id=1, source_target_pairs={{0,6},{2,0},{4,2},{6,4},{1,7},{3,1},{5,3},{7,5},{8,14},{10,8},{12,... | collective-permute-start | bytes 786440 | tf_op jit(solution)/shard_map/ppermute | solution.py:373
  162.0 1.3 copy-start.7
  164.0 15.4 %all-to-all-start.3 = ((bf16[8,8,128]{2,1,0:T(8,128)(2,1)}), bf16[8,8,128]{2,1,0:T(8,128)(2,1)S(1)}, u32[]{:S(2)}, u32[]{:S(2)}) async-start(bf16[8,8,128]{2,1,0:T(8,128)(2,1)} %fusion), calls=%async_computation.3 | async-start | bytes 32768 | tf_op jit(solution)/shard_map/all_to_all | solution.py:401

commit v3 on v1

--- a/solution.py
+++ b/solution.py
@@ -207,7 +207,95 @@
     )(shifts, position, tile, tb, side, corner)
 
 
-def join_kernel(slot_ref, got_ref, denom_ref, joined_ref, quads_ref, acc_ref, sum_ref, mean_ref):
+def exchange_kernel(count_y, count_x, send_ref, code_ref, got_ref, got_code_ref, sems, code_sems, own_sems):
+    devices = count_y * count_x
+    capacity = send_ref.shape[0] // devices
+    me = lax.axis_index("ty") * count_x + lax.axis_index("tx")
+    barrier = pltpu.get_barrier_semaphore()
+
+    def at(peer):
+        return (peer // count_x, peer % count_x)
+
+    def greet(d, carry):
+        pl.semaphore_signal(
+            barrier, inc=1, device_id=at((me + d) % devices), device_id_type=pl.DeviceIdType.MESH
+        )
+        return carry
+
+    lax.fori_loop(1, devices, greet, 0)
+    pl.semaphore_wait(barrier, devices - 1)
+
+    def copies(source, target, peer):
+        block = pl.ds(source * capacity, capacity)
+        landing = pl.ds(target * capacity, capacity)
+        pieces = pltpu.make_async_remote_copy(
+            src_ref=send_ref.at[block],
+            dst_ref=got_ref.at[landing],
+            send_sem=sems.at[0, source],
+            recv_sem=sems.at[1, target],
+            device_id=at(peer),
+            device_id_type=pl.DeviceIdType.MESH,
+        )
+        codes = pltpu.make_async_remote_copy(
+            src_ref=code_ref.at[source],
+            dst_ref=got_code_ref.at[target],
+            send_sem=code_sems.at[0, source],
+            recv_sem=code_sems.at[1, target],
+            device_id=at(peer),
+            device_id_type=pl.DeviceIdType.MESH,
+        )
+        return pieces, codes
+
+    def start(d, carry):
+        peer = (me + d) % devices
+        for copy in copies(peer, me, peer):
+            copy.start()
+        return carry
+
+    lax.fori_loop(1, devices, start, 0)
+    mine = pl.ds(me * capacity, capacity)
+    own = pltpu.make_async_copy(send_ref.at[mine], got_ref.at[mine], own_sems.at[0])
+    own_code = pltpu.make_async_copy(code_ref.at[me], got_code_ref.at[me], own_sems.at[1])
+    own.start()
+    own_code.start()
+    own.wait()
+    own_code.wait()
+
+    def finish(d, carry):
+        peer = (me + d) % devices
+        for copy in copies(peer, peer, peer):
+            copy.wait_send()
+            copy.wait_recv()
+        return carry
+
+    lax.fori_loop(1, devices, finish, 0)
+
+
+def exchange(send, codes, count_y, count_x):
+    devices = count_y * count_x
+    vmem = pl.BlockSpec(memory_space=pltpu.VMEM)
+    return pl.pallas_call(
+        functools.partial(exchange_kernel, count_y, count_x),
+        out_shape=[
+            jax.ShapeDtypeStruct(send.shape, send.dtype),
+            jax.ShapeDtypeStruct(codes.shape, codes.dtype),
+        ],
+        in_specs=[vmem, vmem],
+        out_specs=[vmem, vmem],
+        scratch_shapes=[
+            pltpu.SemaphoreType.DMA((2, devices)),
+            pltpu.SemaphoreType.DMA((2, devices)),
+            pltpu.SemaphoreType.DMA((2,)),
+        ],
+        name="exchange",
+        compiler_params=pltpu.CompilerParams(
+            collective_id=0, has_side_effects=True, vmem_limit_bytes=24 * 2**20
+        ),
+        cost_estimate=pl.CostEstimate(flops=0, bytes_accessed=2**23, transcendentals=0),
+    )(send, codes)
+
+
+def join_kernel(slot_ref, code_ref, patch_ref, got_ref, joined_ref, quads_ref, acc_ref, sum_ref, mean_ref, denom_ref):
     acc_ref[...] = jnp.zeros_like(acc_ref)
     step = 8
 
@@ -218,6 +306,14 @@
         return carry
 
     lax.fori_loop(0, got_ref.shape[0] // step, add, 0)
+    codes = code_ref[...]
+    number = codes.shape[1]
+    grid = patch_ref.shape[1]
+    slot_marks = (codes % CODE == iota((SLOTS, number), 0)).astype(BF16)
+    place_marks = (codes // CODE == iota((grid, number), 0)).astype(BF16)
+    counts = mm_t(slot_marks, place_marks).astype(BF16)
+    for y in range(SIDE):
+        denom_ref[pl.ds(y, SLOTS, stride=SIDE), :] = mm(counts, patch_ref[y])
     row = iota((LANES, LANES), 0)
     column = iota((LANES, LANES), 1)
     half = SIDE // 2
@@ -227,7 +323,8 @@
     rows = batch * SIDE
     for c in range(SLOTS // batch):
         part = pl.ds(c * batch, batch)
-        value = (acc_ref[part] / jnp.maximum(denom_ref[part], 1.0)).astype(BF16).reshape(rows, LANES)
+        denom = jnp.maximum(denom_ref[pl.ds(c * rows, rows), :], 1.0)
+        value = (acc_ref[part].reshape(rows, LANES) / denom).astype(BF16)
         mean_ref[...] = value.astype(F32)
         sum_ref[...] = mm(value, pool_one)
         level = (sum_ref[pl.ds(0, rows // 2, stride=2), :] + sum_ref[pl.ds(1, rows // 2, stride=2), :]) * 0.125
@@ -241,7 +338,7 @@
             joined_ref[part, pl.ds(g * high, high), :] = piece.reshape(batch, high, LANES).astype(BF16)
 
 
-def join(slots, got, denom):
+def join(slots, codes, patches, got):
     vmem = pl.BlockSpec(memory_space=pltpu.VMEM)
     smem = pl.BlockSpec(memory_space=pltpu.SMEM)
     return pl.pallas_call(
@@ -250,17 +347,18 @@
             jax.ShapeDtypeStruct((SLOTS, SIDE, LANES), BF16),
             jax.ShapeDtypeStruct((SLOTS * SIDE // 4, LANES), F32),
         ],
-        in_specs=[smem, vmem, vmem],
+        in_specs=[smem, vmem, vmem, vmem],
         out_specs=[vmem, vmem],
         scratch_shapes=[
             pltpu.VMEM((SLOTS + 1, SIDE, LANES), F32),
             pltpu.VMEM((SLOTS // 4 * SIDE, LANES), F32),
             pltpu.VMEM((SLOTS // 4 * SIDE, LANES), F32),
+            pltpu.VMEM((SLOTS * SIDE, LANES), F32),
         ],
         name="join",
         compiler_params=pltpu.CompilerParams(vmem_limit_bytes=32 * 2**20),
         cost_estimate=pl.CostEstimate(flops=10**8, bytes_accessed=2**23, transcendentals=0),
-    )(slots, got, denom)
+    )(slots, codes, patches, got)
 
 
 def assemble(quadrant_blocks):
@@ -271,12 +369,10 @@
 
 def patch_weights(length, depth):
     grid_side = length // SIDE
-    index = jnp.arange(length, dtype=jnp.int32)
-    nearest = jnp.minimum(jnp.minimum(index + 1, length - index), OV).astype(F32)
-    line = (1.0 + 3.0 * nearest / OV).reshape(grid_side, SIDE)
-    across = jnp.tile(line, (1, depth))
-    blend = line[:, None, :, None] * across[None, :, None, :]
-    return blend.astype(BF16).reshape(grid_side * grid_side, SIDE * depth * SIDE)
+    ramps = ramp((1, length), 1, length).reshape(grid_side, SIDE)
+    down = jnp.repeat(ramps, grid_side, axis=0).T
+    across = jnp.tile(ramps, (grid_side, depth))
+    return (down[:, :, None] * across[None]).astype(BF16)
 
 
 def per_device(tiles, shifts, piece_target, coarse_target):
@@ -298,7 +394,8 @@
     send_codes = SLOTS + jnp.sum(
         jnp.where(position[None, :] == rows[:, None], codes[None, :], 0), axis=1
     )
-    got_codes = lax.all_to_all(send_codes, ("ty", "tx"), split_axis=0, concat_axis=0, tiled=True)
+    send_codes = jnp.broadcast_to(send_codes.reshape(devices, 1, capacity), (devices, 8, capacity))
+    send_codes = jnp.pad(send_codes, ((0, 0), (0, 0), (0, LANES - capacity)))
 
     top = shifted(tile[:, length - H :, :], "ty", 1)
     bottom = shifted(tile[:, :H, :], "ty", -1)
@@ -309,22 +406,15 @@
     right = shifted(first.transpose(0, 2, 1), "tx", -1)
     side = jnp.concatenate([left, right], axis=1)
     right_bins, left_bins, bottom_bins, top_bins = all_bins(tile)
-    position, got_codes, left_bins, top_bins = lax.optimization_barrier(
-        (position, got_codes, left_bins, top_bins)
-    )
     next_left = shifted(left_bins, "tx", -1)
     next_top = shifted(top_bins, "ty", -1)
     send = make_pieces(
         shifts[0, 0], position, tile, tb, side[:, :, :length], side[:, :, length:], devices * capacity
     )
-    got = lax.all_to_all(send, ("ty", "tx"), split_axis=0, concat_axis=0, tiled=True)
-
     corr_right, corr_below = phase_surfaces(right_bins, next_left, bottom_bins, next_top)
-    slots = got_codes % CODE
-    slot_marks = slots[None, :] == jnp.arange(SLOTS, dtype=jnp.int32)[:, None]
-    place_marks = (got_codes // CODE)[:, None] == order[None, :]
-    counts = mm(slot_marks.astype(BF16), place_marks.astype(BF16)).astype(BF16)
-    denom = mm(counts, patch_weights(length, depth)).reshape(SLOTS, SIDE, LANES)
+    patches = patch_weights(length, depth)
+    got, got_codes = exchange(send, send_codes, count_y, count_x)
+    codes = got_codes[:, 0, :capacity].reshape(-1)
 
     coarse_ids = coarse_target[0, 0]
     owner = coarse_ids // SLOTS
@@ -334,10 +424,7 @@
     coarse_pos = owner * per_peer + jnp.sum(ahead.astype(jnp.int32), axis=1)
     ordering = (coarse_pos[None, :] == number[:, None]).astype(BF16)
     locals_ = jnp.broadcast_to((coarse_ids % SLOTS).astype(BF16)[:, None], (SLOTS, SLOTS))
-    got, denom, slots, ordering, locals_, corr_right, corr_below = lax.optimization_barrier(
-        (got, denom, slots, ordering, locals_, corr_right, corr_below)
-    )
-    joined, quads = join(slots, got, denom)
+    joined, quads = join(codes % CODE, codes[None, :], patches, got)
     joined = joined.reshape(SLOTS, depth * SIDE * SIDE)
     flat = quads[:, : SIDE // 4].astype(BF16).reshape(SLOTS, -1)
     send_quads = mm(ordering, jnp.concatenate([flat, locals_], axis=1)).astype(BF16)

time: 169 us -> 170 us (level)
  Pallas kernels: 20.5 us -> 118 us
  waiting for transfers between devices: 82.7 us -> 5.5 us
  starting transfers between devices: 36.6 us -> 26.1 us
  local copies, waits for them, and re-layouts: 20.8 us -> 15.2 us
    pallas_call x0 -> x1, Pallas kernels: none -> 97.3 us  [exchange(): pl.pallas_call(functools.partial(exchange_kernel, count_y, count_x), out_...]
    all_to_all x2 -> x0, waiting for transfers between devices: 67.8 us -> none  [the longest x1 67.8 us: per_device(): lax.all_to_all(send, ('ty', 'tx'), split_axis=0, concat_axis=0, tiled=True)]
    all_to_all x2 -> x0, starting transfers between devices: 18.7 us -> none  [the longest x1 11.4 us: per_device(): lax.all_to_all(send, ('ty', 'tx'), split_axis=0, concat_axis=0, tiled=True)]
    all_to_all x1, starting transfers between devices: 5.76 us -> 13.6 us  [per_device(): lax.all_to_all(send_quads, 'tx', split_axis=0, concat_axis=0, tiled=True)]
    all_to_all x1, waiting for transfers between devices: 5.57 us -> 0.01 us  [per_device(): lax.all_to_all(send_quads, 'tx', split_axis=0, concat_axis=0, tiled=True)]
    ppermute x6, waiting for transfers between devices: 9.34 us -> 5.5 us  [shifted(): lax.ppermute(value, axis, [(source, source + steps) for source in range(f...]
    dot_general x1 -> x0, local copies, waits for them, and re-layouts: 3.31 us -> none  [mm(): return jnp.dot(a, b, preferred_element_type=F32)]
    slice x1 -> x4, local copies, waits for them, and re-layouts: 0.01 us -> 1.78 us  [per_device(): first = jnp.concatenate([tile[:, :, :H], tb[:, :, :H]], axis=1)]
  transfers between devices with their start and end apart: 9 -> 7, of which waited for: 3 -> 2; matrix products, arithmetic and copies ran while one was open for 12% -> 7% of each run, Pallas kernels for 4% -> 69%
where the time goes in v3:
time: 170 us
  Pallas kernels  118 us (69%)
  starting transfers between devices  26.1 us (15%)
  local copies, waits for them, and re-layouts  15.2 us (9%)
  waiting for transfers between devices  5.5 us (3%)
  other arithmetic  3.19 us (2%)
    pallas_call x1, Pallas kernels, exchange(): pl.pallas_call(functools.partial(exchange_kernel, count_y, count_x), out_...  97.3 us
    all_to_all x1, starting transfers between devices, per_device(): lax.all_to_all(send_quads, 'tx', split_axis=0, concat_axis=0, tiled=True)  13.6 us
    ppermute x6, starting transfers between devices, shifted(): lax.ppermute(value, axis, [(source, source + steps) for source in range(f...  12.5 us
    unnamed x20, local copies, waits for them, and re-layouts  7.44 us
    pallas_call x1, Pallas kernels, make_pieces(): pl.pallas_call(pieces_kernel, out_shape=jax.ShapeDtypeStruct((rows, SIDE,...  7.14 us
    pallas_call x1, Pallas kernels, join(): pl.pallas_call(join_kernel, out_shape=[jax.ShapeDtypeStruct((SLOTS, SIDE,...  6.18 us
    ppermute x6, waiting for transfers between devices, shifted(): lax.ppermute(value, axis, [(source, source + steps) for source in range(f...  5.5 us
    pallas_call x1, Pallas kernels, phase_surfaces(): pl.pallas_call(phase_kernel, out_shape=[jax.ShapeDtypeStruct((16, columns...  3.94 us
  transfers between devices with their start and end apart: 7, of which 2 were waited for; matrix products, arithmetic and copies ran while one was open for 7% of the time, Pallas kernels for 69%

profile of v3, /device:TPU:0, one launch (start us, length us, event | category | flops | bytes accessed | tf_op | source)
XLA Modules:
  0.0 169.5 jit_solution(3166927835966497705)
XLA Ops:
  0.6 0.0 copy-start.6
  0.6 0.0 copy-start.7
  0.7 0.8 fusion.26
  1.4 2.3 %collective-permute-start = (bf16[4,8,512]{2,1,0:T(8,128)(2,1)S(1)}, bf16[4,8,512]{2,1,0:T(8,128)(2,1)S(1)}, u32[]{:S(2)}, u32[]{:S(2)}) collective-permute-start(bf16[4,8,512]{2,1,0:T(8,128)(2,1)S(1)} %get-tuple-element.43), channel_id=1, source_target_pairs={{0,8},{8,16},{16,24},{1,9},{9,17},{17,25},{2,10},{10,18},{18,26},{... | collective-permute-start | bytes 98312 | tf_op jit(solution)/shard_map/ppermute | solution.py:25
  3.8 1.3 collective-permute-start.1
  5.1 3.2 %bins.1 = (f32[12,128]{1,0:T(8,128)}, f32[12,128]{1,0:T(8,128)}, f32[12,128]{1,0:T(8,128)}, f32[12,128]{1,0:T(8,128)}) custom-call(bf16[4,512,512]{2,1,0:T(8,128)(2,1)} %bitcast.38), custom_call_target="tpu_custom_call" | custom-call | flops 100000000 | bytes 2097152 | tf_op jit(solution)/shard_map/bins/pallas_call | solution.py:68
  8.3 1.4 collective-permute-start.4
  9.7 1.3 collective-permute-start.5
  11.0 1.4 fusion.25
  12.5 0.9 sine_multiply_fusion
  13.4 0.0 copy-done.6
  13.4 0.2 convert_reduce_fusion
  13.6 0.2 select_reduce_fusion
  13.8 0.1 tile.2
  13.9 0.3 mul.122
  14.1 0.1 copy.34
  14.2 0.0 copy-done.7
  14.2 0.2 convert_reduce_fusion.2
  14.4 1.4 multiply_convert_fusion.patch_ref
  15.8 0.1 cosine_multiply_fusion.1
  15.9 0.2 copy.30
  16.0 0.2 copy.32
  16.2 0.1 add.159
  16.4 0.0 collective-permute-done
  16.4 0.0 collective-permute-done.1
  16.4 0.1 fusion.28
  16.5 0.1 copy.31
  16.6 4.9 %collective-permute-start.2 = (bf16[4,8,528]{2,1,0:T(8,128)(2,1)S(1)}, bf16[4,8,528]{2,1,0:T(8,128)(2,1)S(1)}, u32[]{:S(2)}, u32[]{:S(2)}) collective-permute-start(bf16[4,8,528]{2,1,0:T(8,128)(2,1)S(1)} %maximum_bitcast_fusion), channel_id=1, source_target_pairs={{0,1},{1,2},{2,3},{3,4},{4,5},{5,6},{6,7},{8,9},{9,10},{10,11},{11... | collective-permute-start | bytes 101384 | tf_op jit(solution)/shard_map/ppermute | solution.py:25
  21.5 0.1 copy.33
  21.6 1.3 collective-permute-start.3
  22.9 0.3 collective-permute-done.2
  23.1 5.2 %collective-permute-done.3 = bf16[4,8,528]{2,1,0:T(8,128)(2,1)S(1)} collective-permute-done((bf16[4,8,528]{2,1,0:T(8,128)(2,1)S(1)}, bf16[4,8,528]{2,1,0:T(8,128)(2,1)S(1)}, u32[]{:S(2)}, u32[]{:S(2)}) %collective-permute-start.3) | collective-permute-done | bytes 33824 | tf_op jit(solution)/shard_map/ppermute | solution.py:25
  28.4 0.0 copy-start
  28.4 1.6 copy-done
  30.0 7.1 %pieces.1.send_ref = bf16[512,32,128]{2,1,0:T(8,128)(2,1)S(1)} custom-call(s32[2]{0:T(128)S(1)} %bitcast.42, s32[256]{0:T(256)S(1)} %multiply_add_fusion.1.pos_ref, bf16[4,512,512]{2,1,0:T(8,128)(2,1)S(1)} %bitcast.40, bf16[4,16,512]{2,1,0:T(8,128)(2,1)S(1)} %constant_dynamic-update-slice_fusion.tb_ref, bf16[4,16,512]{2,1,0:T(8,128)(2,1)S(1)} %slice.63.side_ref, ...), custom_call_target="tpu_custom_call" | custom-call | flops 2000000000 | bytes 8388608 | tf_op jit(solution)/shard_map/pieces/pallas_call | solution.py:198
  37.1 97.3 %exchange.1 = (bf16[512,32,128]{2,1,0:T(8,128)(2,1)S(1)}, s32[32,8,128]{2,1,0:T(8,128)S(1)}) custom-call(bf16[512,32,128]{2,1,0:T(8,128)(2,1)S(1)} %pieces.1.send_ref, s32[32,8,128]{2,1,0:T(8,128)S(1)} %pad.24.code_ref), custom_call_target="tpu_custom_call" | custom-call | bytes 8388608 | tf_op jit(solution)/shard_map/exchange/pallas_call | solution.py:277
  134.4 0.0 copy-start.1
  134.4 1.9 %copy-done.1 = bf16[512,32,128]{2,1,0:T(8,128)(2,1)} copy-done((bf16[512,32,128]{2,1,0:T(8,128)(2,1)}, bf16[512,32,128]{2,1,0:T(8,128)(2,1)S(1)}, u32[]{:S(2)}) %copy-start.1) | copy-done | bytes 4194328
  136.4 0.1 reshape_squeeze.3
  136.5 0.1 broadcast_in_dim_reshape_squeeze.3.code_ref
  136.6 2.2 %copy-done.2 = bf16[512,32,128]{2,1,0:T(8,128)(2,1)S(1)} copy-done((bf16[512,32,128]{2,1,0:T(8,128)(2,1)S(1)}, bf16[512,32,128]{2,1,0:T(8,128)(2,1)}, u32[]{:S(2)}) %copy-start.2) | copy-done | bytes 4194328
  138.8 6.2 %join.1 = (bf16[64,32,128]{2,1,0:T(8,128)(2,1)S(1)}, f32[512,128]{1,0:T(8,128)S(1)}) custom-call(s32[512]{0:T(512)S(1)} %add_select_fusion.2.slot_ref, s32[1,512]{1,0:T(1,128)S(1)} %broadcast_in_dim_reshape_squeeze.3.code_ref, bf16[32,256,128]{2,1,0:T(8,128)(2,1)S(1)} %multiply_convert_fusion.patch_ref, bf16[512,32,128]{2,1,0:T(8,128)(2,1)S(1)} %copy-done.2), custom_call_target="tpu_custom_call" | custom-call | flops 100000000 | bytes 8388608 | tf_op jit(solution)/shard_map/join/pallas_call | solution.py:344
  145.0 0.1 reshape.256
  145.1 0.1 broadcast_in_dim.22
  145.2 0.8 fusion
  146.0 13.6 %all-to-all-start = ((bf16[8,8,128]{2,1,0:T(8,128)(2,1)}), bf16[8,8,128]{2,1,0:T(8,128)(2,1)S(1)}, u32[]{:S(2)}, u32[]{:S(2)}) async-start(bf16[8,8,128]{2,1,0:T(8,128)(2,1)} %fusion), calls=%async_computation | async-start | bytes 32768 | tf_op jit(solution)/shard_map/all_to_all | solution.py:431
  159.6 0.1 sine_multiply_fusion.1
  159.6 0.6 pad.27.r_ref
  160.2 0.0 copy-done.4
  160.2 0.6 pad.29.b_ref
  160.8 0.6 pad.25.ca_ref
  161.4 0.6 pad.26.sa_ref
  162.0 0.0 collective-permute-done.4
  162.1 0.6 pad.28.l_ref
  162.6 0.0 collective-permute-done.5
  162.7 0.6 pad.30.t_ref
  163.3 3.9 %phase.1 = (f32[16,128]{1,0:T(8,128)}, f32[16,128]{1,0:T(8,128)}) custom-call(f32[16,16]{1,0:T(8,128)} %pad.25.ca_ref, f32[16,16]{1,0:T(8,128)} %pad.26.sa_ref, f32[128,128]{1,0:T(8,128)} %get-tuple-element.53.cb_ref, f32[128,128]{1,0:T(8,128)} %get-tuple-element.52.sb_ref, f32[16,128]{1,0:T(8,128)} %pad.27.r_ref, f32[16,128]{1,0:T(8,128)} %pad.28.l_ref, ...), custom_call_target="tpu_custom_call" | custom-call | flops 100000000 | bytes 262144 | tf_op jit(solution)/shard_map/phase/pallas_call | solution.py:116
  167.2 1.0 copy.39
  168.2 0.0 all-to-all-done
  168.2 0.2 convert_reduce_fusion.1
  168.4 0.1 convolution_convert_fusion
  168.5 0.1 convert_element_type.83
  168.7 0.2 copy.35
  168.9 0.7 copy.36
  (26 shorter events, 0.3 us)
Async XLA Ops:
  0.6 12.8 %copy-start.6 = (s32[1,1,256]{2,1,0:T(1,128)S(1)}, s32[1,1,256]{2,1,0:T(1,128)}, u32[]{:S(2)}) copy-start(s32[1,1,256]{2,1,0:T(1,128)} %param.6) | copy-start | bytes 3076
  0.6 13.6 %copy-start.7 = (s32[1,1,64]{2,1,0:T(1,128)S(1)}, s32[1,1,64]{2,1,0:T(1,128)}, u32[]{:S(2)}) copy-start(s32[1,1,64]{2,1,0:T(1,128)} %param.7) | copy-start | bytes 772
  1.4 14.9 %collective-permute-start = (bf16[4,8,512]{2,1,0:T(8,128)(2,1)S(1)}, bf16[4,8,512]{2,1,0:T(8,128)(2,1)S(1)}, u32[]{:S(2)}, u32[]{:S(2)}) collective-permute-start(bf16[4,8,512]{2,1,0:T(8,128)(2,1)S(1)} %get-tuple-element.43), channel_id=1, source_target_pairs={{0,8},{8,16},{16,24},{1,9},{9,17},{17,25},{2,10},{10,18},{18,26},{... | collective-permute-start | bytes 98312 | tf_op jit(solution)/shard_map/ppermute | solution.py:25
  3.8 12.6 %collective-permute-start.1 = (bf16[4,8,512]{2,1,0:T(8,128)(2,1)S(1)}, bf16[4,8,512]{2,1,0:T(8,128)(2,1)S(1)}, u32[]{:S(2)}, u32[]{:S(2)}) collective-permute-start(bf16[4,8,512]{2,1,0:T(8,128)(2,1)S(1)} %get-tuple-element.42), channel_id=1, source_target_pairs={{8,0},{16,8},{24,16},{9,1},{17,9},{25,17},{10,2},{18,10},{26,18},{... | collective-permute-start | bytes 98312 | tf_op jit(solution)/shard_map/ppermute | solution.py:25
  8.3 20.1 %copy-start.3 = (s32[1,1,2]{2,1,0:T(1,128)S(1)}, s32[1,1,2]{2,1,0:T(1,128)}, u32[]{:S(2)}) copy-start(s32[1,1,2]{2,1,0:T(1,128)} %param.5) | copy-start | bytes 28
  8.3 153.8 %collective-permute-start.4 = (f32[12,128]{1,0:T(8,128)}, f32[12,128]{1,0:T(8,128)S(1)}, u32[]{:S(2)}, u32[]{:S(2)}) collective-permute-start(f32[12,128]{1,0:T(8,128)} %get-tuple-element.19), channel_id=1, source_target_pairs={{1,0},{2,1},{3,2},{4,3},{5,4},{6,5},{7,6},{9,8},{10,9},{11,10},{12... | collective-permute-start | bytes 18440 | tf_op jit(solution)/shard_map/ppermute | solution.py:25
  9.7 152.9 %collective-permute-start.5 = (f32[12,128]{1,0:T(8,128)}, f32[12,128]{1,0:T(8,128)S(1)}, u32[]{:S(2)}, u32[]{:S(2)}) collective-permute-start(f32[12,128]{1,0:T(8,128)} %get-tuple-element.21), channel_id=1, source_target_pairs={{8,0},{16,8},{24,16},{9,1},{17,9},{25,17},{10,2},{18,10},{26,18},{... | collective-permute-start | bytes 18440 | tf_op jit(solution)/shard_map/ppermute | solution.py:25
  16.6 6.5 %collective-permute-start.2 = (bf16[4,8,528]{2,1,0:T(8,128)(2,1)S(1)}, bf16[4,8,528]{2,1,0:T(8,128)(2,1)S(1)}, u32[]{:S(2)}, u32[]{:S(2)}) collective-permute-start(bf16[4,8,528]{2,1,0:T(8,128)(2,1)S(1)} %maximum_bitcast_fusion), channel_id=1, source_target_pairs={{0,1},{1,2},{2,3},{3,4},{4,5},{5,6},{6,7},{8,9},{9,10},{10,11},{11... | collective-permute-start | bytes 101384 | tf_op jit(solution)/shard_map/ppermute | solution.py:25
  21.6 6.8 %collective-permute-start.3 = (bf16[4,8,528]{2,1,0:T(8,128)(2,1)S(1)}, bf16[4,8,528]{2,1,0:T(8,128)(2,1)S(1)}, u32[]{:S(2)}, u32[]{:S(2)}) collective-permute-start(bf16[4,8,528]{2,1,0:T(8,128)(2,1)S(1)} %maximum_bitcast_fusion.1), channel_id=1, source_target_pairs={{1,0},{2,1},{3,2},{4,3},{5,4},{6,5},{7,6},{9,8},{10,9},{11,10},{12... | collective-permute-start | bytes 101384 | tf_op jit(solution)/shard_map/ppermute | solution.py:25
  28.4 1.6 copy-start
  134.4 2.0 %copy-start.1 = (bf16[512,32,128]{2,1,0:T(8,128)(2,1)}, bf16[512,32,128]{2,1,0:T(8,128)(2,1)S(1)}, u32[]{:S(2)}) copy-start(bf16[512,32,128]{2,1,0:T(8,128)(2,1)S(1)} %get-tuple-element.15.got_ref) | copy-start | bytes 12582916
  136.4 23.3 %copy-start.5 = (f32[12,128]{1,0:T(8,128)S(1)}, f32[12,128]{1,0:T(8,128)}, u32[]{:S(2)}) copy-start(f32[12,128]{1,0:T(8,128)} %get-tuple-element.18) | copy-start | bytes 18436
  136.4 23.9 %copy-start.4 = (f32[12,128]{1,0:T(8,128)S(1)}, f32[12,128]{1,0:T(8,128)}, u32[]{:S(2)}) copy-start(f32[12,128]{1,0:T(8,128)} %get-tuple-element.20) | copy-start | bytes 18436
  136.6 2.2 %copy-start.2 = (bf16[512,32,128]{2,1,0:T(8,128)(2,1)S(1)}, bf16[512,32,128]{2,1,0:T(8,128)(2,1)}, u32[]{:S(2)}) copy-start(bf16[512,32,128]{2,1,0:T(8,128)(2,1)} %copy-done.1) | copy-start | bytes 12582916
  146.0 22.2 %all-to-all-start = ((bf16[8,8,128]{2,1,0:T(8,128)(2,1)}), bf16[8,8,128]{2,1,0:T(8,128)(2,1)S(1)}, u32[]{:S(2)}, u32[]{:S(2)}) async-start(bf16[8,8,128]{2,1,0:T(8,128)(2,1)} %fusion), calls=%async_computation | async-start | bytes 32768 | tf_op jit(solution)/shard_map/all_to_all | solution.py:431

commit v4 on v3

--- a/solution.py
+++ b/solution.py
@@ -41,7 +41,7 @@
     return lax.dot_general(a, b, (((1,), (1,)), ((), ())), preferred_element_type=F32)
 
 
-def bins_kernel(tile_ref, right_ref, left_ref, bottom_ref, top_ref):
+def bins_kernel(tile_ref, after_ref, right_ref, left_ref, bottom_ref, top_ref):
     depth, length, _ = tile_ref.shape
     bins = OV // 4
     scale = 1.0 / math.sqrt(16.0 * depth)
@@ -61,18 +61,18 @@
         ref[...] = highest(value, pool)[:bins] * scale
 
 
-def all_bins(tile):
+def all_bins(tile, after):
     length = tile.shape[1]
     shape = jax.ShapeDtypeStruct((OV // 4, length // 4), F32)
     vmem = pl.BlockSpec(memory_space=pltpu.VMEM)
     return pl.pallas_call(
         bins_kernel,
         out_shape=[shape] * 4,
-        in_specs=[vmem],
+        in_specs=[vmem, vmem],
         out_specs=[vmem] * 4,
         name="bins",
         cost_estimate=pl.CostEstimate(flops=10**8, bytes_accessed=2**21, transcendentals=0),
-    )(tile)
+    )(tile, after)
 
 
 def dft_tables(length):
@@ -202,7 +202,7 @@
         out_specs=vmem,
         scratch_shapes=[pltpu.VMEM(tile.shape, F32)],
         name="pieces",
-        compiler_params=pltpu.CompilerParams(vmem_limit_bytes=40 * 2**20),
+        compiler_params=pltpu.CompilerParams(vmem_limit_bytes=24 * 2**20),
         cost_estimate=pl.CostEstimate(flops=2 * 10**9, bytes_accessed=2**23, transcendentals=0),
     )(shifts, position, tile, tb, side, corner)
 
@@ -281,7 +281,7 @@
             jax.ShapeDtypeStruct(codes.shape, codes.dtype),
         ],
         in_specs=[vmem, vmem],
-        out_specs=[vmem, vmem],
+        out_specs=[pl.BlockSpec(memory_space=pl.ANY), vmem],
         scratch_shapes=[
             pltpu.SemaphoreType.DMA((2, devices)),
             pltpu.SemaphoreType.DMA((2, devices)),
@@ -289,7 +289,7 @@
         ],
         name="exchange",
         compiler_params=pltpu.CompilerParams(
-            collective_id=0, has_side_effects=True, vmem_limit_bytes=24 * 2**20
+            collective_id=0, has_side_effects=True, vmem_limit_bytes=12 * 2**20
         ),
         cost_estimate=pl.CostEstimate(flops=0, bytes_accessed=2**23, transcendentals=0),
     )(send, codes)
@@ -356,7 +356,7 @@
             pltpu.VMEM((SLOTS * SIDE, LANES), F32),
         ],
         name="join",
-        compiler_params=pltpu.CompilerParams(vmem_limit_bytes=32 * 2**20),
+        compiler_params=pltpu.CompilerParams(vmem_limit_bytes=16 * 2**20),
         cost_estimate=pl.CostEstimate(flops=10**8, bytes_accessed=2**23, transcendentals=0),
     )(slots, codes, patches, got)
 
@@ -367,9 +367,10 @@
     return shaped.reshape(count // 4, 4 * height * width)
 
 
-def patch_weights(length, depth):
+def patch_weights(length, depth, after):
     grid_side = length // SIDE
     ramps = ramp((1, length), 1, length).reshape(grid_side, SIDE)
+    ramps, _ = lax.optimization_barrier((ramps, after))
     down = jnp.repeat(ramps, grid_side, axis=0).T
     across = jnp.tile(ramps, (grid_side, depth))
     return (down[:, :, None] * across[None]).astype(BF16)
@@ -402,17 +403,18 @@
     tb = jnp.concatenate([top, bottom], axis=1)
     last = jnp.concatenate([tile[:, :, length - H :], tb[:, :, length - H :]], axis=1)
     first = jnp.concatenate([tile[:, :, :H], tb[:, :, :H]], axis=1)
-    left = shifted(last.transpose(0, 2, 1), "tx", 1)
-    right = shifted(first.transpose(0, 2, 1), "tx", -1)
+    last, first = last.transpose(0, 2, 1), first.transpose(0, 2, 1)
+    left = shifted(last, "tx", 1)
+    right = shifted(first, "tx", -1)
     side = jnp.concatenate([left, right], axis=1)
-    right_bins, left_bins, bottom_bins, top_bins = all_bins(tile)
+    right_bins, left_bins, bottom_bins, top_bins = all_bins(tile, first)
     next_left = shifted(left_bins, "tx", -1)
     next_top = shifted(top_bins, "ty", -1)
     send = make_pieces(
         shifts[0, 0], position, tile, tb, side[:, :, :length], side[:, :, length:], devices * capacity
     )
     corr_right, corr_below = phase_surfaces(right_bins, next_left, bottom_bins, next_top)
-    patches = patch_weights(length, depth)
+    patches = patch_weights(length, depth, tb)
     got, got_codes = exchange(send, send_codes, count_y, count_x)
     codes = got_codes[:, 0, :capacity].reshape(-1)
 

time: 170 us -> 175 us (1.029)
  Pallas kernels: 118 us -> 125 us
  waiting for transfers between devices: 5.5 us -> 3.05 us
  other arithmetic: 3.19 us -> 5.25 us
    pallas_call x1, Pallas kernels: 97.3 us -> 104 us  [exchange(): pl.pallas_call(functools.partial(exchange_kernel, count_y, count_x), out_...]
    ppermute x6, waiting for transfers between devices: 5.5 us -> 3.05 us  [shifted(): lax.ppermute(value, axis, [(source, source + steps) for source in range(f...]
    slice x4 -> x1, local copies, waits for them, and re-layouts: 1.78 us -> 0.01 us  [per_device(): first = jnp.concatenate([tile[:, :, :H], tb[:, :, :H]], axis=1)]
    unnamed x20 -> x26, local copies, waits for them, and re-layouts: 7.44 us -> 8.66 us
  transfers between devices with their start and end apart: 7 -> 7, of which waited for: 2 -> 1; matrix products, arithmetic and copies ran while one was open for 7% -> 7% of each run, Pallas kernels for 69% -> 71%
where the time goes in v4:
time: 175 us; the launch traced here: 174 us
  Pallas kernels  125 us (71%)
  starting transfers between devices  24.6 us (14%)
  local copies, waits for them, and re-layouts  15 us (9%)
  other arithmetic  5.25 us (3%)
  waiting for transfers between devices  3.05 us (2%)
    pallas_call x1, Pallas kernels, exchange(): pl.pallas_call(functools.partial(exchange_kernel, count_y, count_x), out_...  104 us
    all_to_all x1, starting transfers between devices, per_device(): lax.all_to_all(send_quads, 'tx', split_axis=0, concat_axis=0, tiled=True)  12.4 us
    ppermute x6, starting transfers between devices, shifted(): lax.ppermute(value, axis, [(source, source + steps) for source in range(f...  12.2 us
    unnamed x26, local copies, waits for them, and re-layouts  8.66 us
    pallas_call x1, Pallas kernels, make_pieces(): pl.pallas_call(pieces_kernel, out_shape=jax.ShapeDtypeStruct((rows, SIDE,...  7.15 us
    pallas_call x1, Pallas kernels, join(): pl.pallas_call(join_kernel, out_shape=[jax.ShapeDtypeStruct((SLOTS, SIDE,...  6.15 us
    pallas_call x1, Pallas kernels, phase_surfaces(): pl.pallas_call(phase_kernel, out_shape=[jax.ShapeDtypeStruct((16, columns...  3.94 us
  transfers between devices with their start and end apart: 7, of which 1 were waited for; matrix products, arithmetic and copies ran while one was open for 7% of the time, Pallas kernels for 71%

profile of v4, /device:TPU:0, one launch (start us, length us, event | category | flops | bytes accessed | tf_op | source)
XLA Modules:
  0.0 174.3 jit_solution(1361543389105081508)
XLA Ops:
  0.6 2.8 %copy.39 = bf16[1,1,4,512,512]{3,4,2,1,0:T(8,128)(2,1)S(1)} copy(bf16[1,1,4,512,512]{4,3,2,1,0:T(8,128)(2,1)} %param.4) | data formatting | bytes 4194304 | tf_op args[0]
  3.4 0.0 copy-start.9
  3.4 0.0 copy-start.10
  3.5 1.2 fusion.28
  4.7 2.4 %collective-permute-start = (bf16[4,8,512]{1,2,0:T(8,128)(2,1)}, bf16[4,8,512]{1,2,0:T(8,128)(2,1)S(1)}, u32[]{:S(2)}, u32[]{:S(2)}) collective-permute-start(bf16[4,8,512]{1,2,0:T(8,128)(2,1)} %get-tuple-element.44), channel_id=1, source_target_pairs={{0,8},{8,16},{16,24},{1,9},{9,17},{17,25},{2,10},{10,18},{18,26},{... | collective-permute-start | bytes 98312 | tf_op jit(solution)/shard_map/ppermute | solution.py:25
  7.0 1.3 collective-permute-start.1
  8.4 0.9 sine_multiply_fusion
  9.3 0.0 copy-done.9
  9.3 0.2 convert_reduce_fusion
  9.5 0.2 select_reduce_fusion
  9.7 0.0 copy-done.10
  9.7 0.2 convert_reduce_fusion.2
  9.9 0.1 cosine_multiply_fusion.1
  10.0 0.1 add.140
  10.1 0.0 collective-permute-done
  10.1 3.0 %collective-permute-done.1 = bf16[4,8,512]{1,2,0:T(8,128)(2,1)S(1)} collective-permute-done((bf16[4,8,512]{1,2,0:T(8,128)(2,1)}, bf16[4,8,512]{1,2,0:T(8,128)(2,1)S(1)}, u32[]{:S(2)}, u32[]{:S(2)}) %collective-permute-start.1) | collective-permute-done | bytes 32800 | tf_op jit(solution)/shard_map/ppermute | solution.py:25
  13.1 0.1 fusion.16
  13.2 1.3 collective-permute-start.3
  14.6 4.5 %collective-permute-start.2 = (bf16[4,8,528]{2,1,0:T(8,128)(2,1)S(1)}, bf16[4,8,528]{2,1,0:T(8,128)(2,1)S(1)}, u32[]{:S(2)}, u32[]{:S(2)}) collective-permute-start(bf16[4,8,528]{2,1,0:T(8,128)(2,1)S(1)} %maximum_bitcast_fusion), channel_id=1, source_target_pairs={{0,1},{1,2},{2,3},{3,4},{4,5},{5,6},{6,7},{8,9},{9,10},{10,11},{11... | collective-permute-start | bytes 101384 | tf_op jit(solution)/shard_map/ppermute | solution.py:25
  19.1 1.1 pad_maximum_fusion
  20.2 0.1 tile.2
  20.3 0.3 mul.121
  20.6 0.1 copy.42
  20.6 0.0 copy-done.6
  20.6 0.0 copy-start.5
  20.7 3.3 %bins.1 = (f32[12,128]{1,0:T(8,128)}, f32[12,128]{1,0:T(8,128)}, f32[12,128]{1,0:T(8,128)}, f32[12,128]{1,0:T(8,128)}) custom-call(bf16[4,512,512]{2,1,0:T(8,128)(2,1)} %bitcast.39, bf16[4,8,528]{2,1,0:T(8,128)(2,1)} %copy-done.6), custom_call_target="tpu_custom_call" | custom-call | flops 100000000 | bytes 2097152 | tf_op jit(solution)/shard_map/bins/pallas_call | solution.py:68
  23.9 1.4 collective-permute-start.4
  25.3 1.3 collective-permute-start.5
  26.6 2.3 %multiply_convert_fusion.patch_ref = bf16[32,256,128]{2,1,0:T(8,128)(2,1)} fusion(f32[256,128]{1,0:T(8,128)S(1)} %mul.121, f32[32,256]{1,0:T(8,128)S(1)} %copy.42), kind=kLoop, calls=%fused_computation | loop fusion | flops 2097152 | bytes 2260992 | tf_op jit(solution)/shard_map/convert_element_type | solution.py:376
  28.9 0.0 copy-done.5
  28.9 0.2 copy.41.tb_ref
  29.1 0.0 collective-permute-done.2
  29.1 0.0 collective-permute-done.3
  29.2 0.0 copy-done
  29.2 0.0 copy-done.4
  29.2 7.1 %pieces.1.send_ref = bf16[512,32,128]{2,1,0:T(8,128)(2,1)S(1)} custom-call(s32[2]{0:T(128)S(1)} %bitcast.42, s32[256]{0:T(256)S(1)} %multiply_add_fusion.1.pos_ref, bf16[4,512,512]{2,1,0:T(8,128)(2,1)S(1)} %bitcast.40, bf16[4,16,512]{2,1,0:T(8,128)(2,1)S(1)} %copy.41.tb_ref, bf16[4,16,512]{2,1,0:T(8,128)(2,1)S(1)} %slice.65.side_ref, ...), custom_call_target="tpu_custom_call" | custom-call | flops 2000000000 | bytes 8388608 | tf_op jit(solution)/shard_map/pieces/pallas_call | solution.py:198
  36.3 0.0 copy-start.1
  36.3 104.1 %exchange.1 = (bf16[512,32,128]{2,1,0:T(8,128)(2,1)S(1)}, s32[32,8,128]{2,1,0:T(8,128)S(1)}) custom-call(bf16[512,32,128]{2,1,0:T(8,128)(2,1)S(1)} %pieces.1.send_ref, s32[32,8,128]{2,1,0:T(8,128)S(1)} %pad.24.code_ref), custom_call_target="tpu_custom_call" | custom-call | bytes 8388608 | tf_op jit(solution)/shard_map/exchange/pallas_call | solution.py:277
  140.4 1.9 %copy-done.2 = bf16[512,32,128]{2,1,0:T(8,128)(2,1)} copy-done((bf16[512,32,128]{2,1,0:T(8,128)(2,1)}, bf16[512,32,128]{2,1,0:T(8,128)(2,1)S(1)}, u32[]{:S(2)}) %copy-start.2) | copy-done | bytes 4194328
  142.4 0.1 reshape_squeeze.3
  142.5 0.1 broadcast_in_dim_reshape_squeeze.3.code_ref
  142.6 2.2 %copy-done.3 = bf16[512,32,128]{2,1,0:T(8,128)(2,1)S(1)} copy-done((bf16[512,32,128]{2,1,0:T(8,128)(2,1)S(1)}, bf16[512,32,128]{2,1,0:T(8,128)(2,1)}, u32[]{:S(2)}) %copy-start.3) | copy-done | bytes 4194328
  144.8 6.1 %join.1 = (bf16[64,32,128]{2,1,0:T(8,128)(2,1)S(1)}, f32[512,128]{1,0:T(8,128)S(1)}) custom-call(s32[512]{0:T(512)S(1)} %add_select_fusion.2.slot_ref, s32[1,512]{1,0:T(1,128)S(1)} %broadcast_in_dim_reshape_squeeze.3.code_ref, bf16[32,256,128]{2,1,0:T(8,128)(2,1)S(1)} %copy-done.1, bf16[512,32,128]{2,1,0:T(8,128)(2,1)S(1)} %copy-done.3), custom_call_target="tpu_custom_call" | custom-call | flops 100000000 | bytes 8388608 | tf_op jit(solution)/shard_map/join/pallas_call | solution.py:344
  151.0 0.1 reshape.242
  151.1 0.1 broadcast_in_dim.22
  151.2 0.8 fusion
  152.0 12.4 %all-to-all-start = ((bf16[8,8,128]{2,1,0:T(8,128)(2,1)}), bf16[8,8,128]{2,1,0:T(8,128)(2,1)S(1)}, u32[]{:S(2)}, u32[]{:S(2)}) async-start(bf16[8,8,128]{2,1,0:T(8,128)(2,1)} %fusion), calls=%async_computation | async-start | bytes 32768 | tf_op jit(solution)/shard_map/all_to_all | solution.py:433
  164.4 0.1 sine_multiply_fusion.1
  164.4 0.6 pad.25.ca_ref
  165.0 0.6 pad.26.sa_ref
  165.7 0.6 pad.27.r_ref
  166.3 0.6 pad.29.b_ref
  166.9 0.0 collective-permute-done.4
  166.9 0.6 pad.28.l_ref
  167.5 0.0 collective-permute-done.5
  167.5 0.6 pad.30.t_ref
  168.1 3.9 %phase.1 = (f32[16,128]{1,0:T(8,128)}, f32[16,128]{1,0:T(8,128)}) custom-call(f32[16,16]{1,0:T(8,128)} %pad.25.ca_ref, f32[16,16]{1,0:T(8,128)} %pad.26.sa_ref, f32[128,128]{1,0:T(8,128)} %get-tuple-element.55.cb_ref, f32[128,128]{1,0:T(8,128)} %get-tuple-element.54.sb_ref, f32[16,128]{1,0:T(8,128)} %pad.27.r_ref, f32[16,128]{1,0:T(8,128)} %pad.28.l_ref, ...), custom_call_target="tpu_custom_call" | custom-call | flops 100000000 | bytes 262144 | tf_op jit(solution)/shard_map/phase/pallas_call | solution.py:116
  172.0 1.0 copy.50
  173.0 0.0 all-to-all-done
  173.0 0.2 convert_reduce_fusion.1
  173.2 0.1 convolution_convert_fusion
  173.3 0.1 convert_element_type.77
  173.5 0.2 copy.43
  173.7 0.7 copy.45
  (29 shorter events, 0.2 us)
Async XLA Ops:
  3.4 5.9 %copy-start.9 = (s32[1,1,256]{2,1,0:T(1,128)S(1)}, s32[1,1,256]{2,1,0:T(1,128)}, u32[]{:S(2)}) copy-start(s32[1,1,256]{2,1,0:T(1,128)} %param.6) | copy-start | bytes 3076
  3.4 6.2 %copy-start.10 = (s32[1,1,64]{2,1,0:T(1,128)S(1)}, s32[1,1,64]{2,1,0:T(1,128)}, u32[]{:S(2)}) copy-start(s32[1,1,64]{2,1,0:T(1,128)} %param.7) | copy-start | bytes 772
  4.7 5.4 %collective-permute-start = (bf16[4,8,512]{1,2,0:T(8,128)(2,1)}, bf16[4,8,512]{1,2,0:T(8,128)(2,1)S(1)}, u32[]{:S(2)}, u32[]{:S(2)}) collective-permute-start(bf16[4,8,512]{1,2,0:T(8,128)(2,1)} %get-tuple-element.44), channel_id=1, source_target_pairs={{0,8},{8,16},{16,24},{1,9},{9,17},{17,25},{2,10},{10,18},{18,26},{... | collective-permute-start | bytes 98312 | tf_op jit(solution)/shard_map/ppermute | solution.py:25
  7.0 6.1 %collective-permute-start.1 = (bf16[4,8,512]{1,2,0:T(8,128)(2,1)}, bf16[4,8,512]{1,2,0:T(8,128)(2,1)S(1)}, u32[]{:S(2)}, u32[]{:S(2)}) collective-permute-start(bf16[4,8,512]{1,2,0:T(8,128)(2,1)} %get-tuple-element.45), channel_id=1, source_target_pairs={{8,0},{16,8},{24,16},{9,1},{17,9},{25,17},{10,2},{18,10},{26,18},{... | collective-permute-start | bytes 98312 | tf_op jit(solution)/shard_map/ppermute | solution.py:25
  13.2 7.4 %copy-start.6 = (bf16[4,8,528]{2,1,0:T(8,128)(2,1)}, bf16[4,8,528]{2,1,0:T(8,128)(2,1)S(1)}, u32[]{:S(2)}) copy-start(bf16[4,8,528]{2,1,0:T(8,128)(2,1)S(1)} %maximum_bitcast_fusion.1.after_ref) | copy-start | bytes 101380
  13.2 15.9 %collective-permute-start.3 = (bf16[4,8,528]{2,1,0:T(8,128)(2,1)S(1)}, bf16[4,8,528]{2,1,0:T(8,128)(2,1)S(1)}, u32[]{:S(2)}, u32[]{:S(2)}) collective-permute-start(bf16[4,8,528]{2,1,0:T(8,128)(2,1)S(1)} %maximum_bitcast_fusion.1.after_ref), channel_id=1, source_target_pairs={{1,0},{2,1},{3,2},{4,3},{5,4},{6,5},{7,6},{9,8},{10,9},{11,10},{12... | collective-permute-start | bytes 101384 | tf_op jit(solution)/shard_map/ppermute | solution.py:25
  14.6 14.5 %collective-permute-start.2 = (bf16[4,8,528]{2,1,0:T(8,128)(2,1)S(1)}, bf16[4,8,528]{2,1,0:T(8,128)(2,1)S(1)}, u32[]{:S(2)}, u32[]{:S(2)}) collective-permute-start(bf16[4,8,528]{2,1,0:T(8,128)(2,1)S(1)} %maximum_bitcast_fusion), channel_id=1, source_target_pairs={{0,1},{1,2},{2,3},{3,4},{4,5},{5,6},{6,7},{8,9},{9,10},{10,11},{11... | collective-permute-start | bytes 101384 | tf_op jit(solution)/shard_map/ppermute | solution.py:25
  20.6 8.3 %copy-start.5 = (bf16[4,16,512]{1,2,0:T(8,128)(2,1)S(1)}, bf16[4,16,512]{1,2,0:T(8,128)(2,1)}, u32[]{:S(2)}) copy-start(bf16[4,16,512]{1,2,0:T(8,128)(2,1)} %pad_maximum_fusion) | copy-start | bytes 196612
  23.9 5.2 %copy-start = (bf16[1,1,4,512,512]{4,3,2,1,0:T(8,128)(2,1)S(1)}, bf16[1,1,4,512,512]{4,3,2,1,0:T(8,128)(2,1)}, u32[]{:S(2)}) copy-start(bf16[1,1,4,512,512]{4,3,2,1,0:T(8,128)(2,1)} %param.4) | copy-start | bytes 6291460
  23.9 5.2 %copy-start.4 = (s32[1,1,2]{2,1,0:T(1,128)S(1)}, s32[1,1,2]{2,1,0:T(1,128)}, u32[]{:S(2)}) copy-start(s32[1,1,2]{2,1,0:T(1,128)} %param.5) | copy-start | bytes 28
  23.9 142.9 %collective-permute-start.4 = (f32[12,128]{1,0:T(8,128)}, f32[12,128]{1,0:T(8,128)S(1)}, u32[]{:S(2)}, u32[]{:S(2)}) collective-permute-start(f32[12,128]{1,0:T(8,128)} %get-tuple-element.21), channel_id=1, source_target_pairs={{1,0},{2,1},{3,2},{4,3},{5,4},{6,5},{7,6},{9,8},{10,9},{11,10},{12... | collective-permute-start | bytes 18440 | tf_op jit(solution)/shard_map/ppermute | solution.py:25
  25.3 142.1 %collective-permute-start.5 = (f32[12,128]{1,0:T(8,128)}, f32[12,128]{1,0:T(8,128)S(1)}, u32[]{:S(2)}, u32[]{:S(2)}) collective-permute-start(f32[12,128]{1,0:T(8,128)} %get-tuple-element.23), channel_id=1, source_target_pairs={{8,0},{16,8},{24,16},{9,1},{17,9},{25,17},{10,2},{18,10},{26,18},{... | collective-permute-start | bytes 18440 | tf_op jit(solution)/shard_map/ppermute | solution.py:25
  36.3 106.3 %copy-start.1 = (bf16[32,256,128]{2,1,0:T(8,128)(2,1)S(1)}, bf16[32,256,128]{2,1,0:T(8,128)(2,1)}, u32[]{:S(2)}) copy-start(bf16[32,256,128]{2,1,0:T(8,128)(2,1)} %multiply_convert_fusion.patch_ref) | copy-start | bytes 6291460
  140.4 2.0 %copy-start.2 = (bf16[512,32,128]{2,1,0:T(8,128)(2,1)}, bf16[512,32,128]{2,1,0:T(8,128)(2,1)S(1)}, u32[]{:S(2)}) copy-start(bf16[512,32,128]{2,1,0:T(8,128)(2,1)S(1)} %get-tuple-element.17.got_ref) | copy-start | bytes 12582916
  142.6 2.2 %copy-start.3 = (bf16[512,32,128]{2,1,0:T(8,128)(2,1)S(1)}, bf16[512,32,128]{2,1,0:T(8,128)(2,1)}, u32[]{:S(2)}) copy-start(bf16[512,32,128]{2,1,0:T(8,128)(2,1)} %copy-done.2) | copy-start | bytes 12582916
  144.8 20.9 %copy-start.8 = (f32[12,128]{1,0:T(8,128)S(1)}, f32[12,128]{1,0:T(8,128)}, u32[]{:S(2)}) copy-start(f32[12,128]{1,0:T(8,128)} %get-tuple-element.20) | copy-start | bytes 18436
  144.8 21.5 %copy-start.7 = (f32[12,128]{1,0:T(8,128)S(1)}, f32[12,128]{1,0:T(8,128)}, u32[]{:S(2)}) copy-start(f32[12,128]{1,0:T(8,128)} %get-tuple-element.22) | copy-start | bytes 18436
  152.0 21.0 %all-to-all-start = ((bf16[8,8,128]{2,1,0:T(8,128)(2,1)}), bf16[8,8,128]{2,1,0:T(8,128)(2,1)S(1)}, u32[]{:S(2)}, u32[]{:S(2)}) async-start(bf16[8,8,128]{2,1,0:T(8,128)(2,1)} %fusion), calls=%async_computation | async-start | bytes 32768 | tf_op jit(solution)/shard_map/all_to_all | solution.py:433

commit v5 on v3

--- a/solution.py
+++ b/solution.py
@@ -247,7 +247,7 @@
         return pieces, codes
 
     def start(d, carry):
-        peer = (me + d) % devices
+        peer = (me + 11 * d) % devices
         for copy in copies(peer, me, peer):
             copy.start()
         return carry

time: 170 us -> 169 us (level)
  starting transfers between devices: 26.1 us -> 22.4 us
  Pallas kernels: 118 us -> 120 us
    all_to_all x1, starting transfers between devices: 13.6 us -> 9.85 us  [per_device(): lax.all_to_all(send_quads, 'tx', split_axis=0, concat_axis=0, tiled=True)]
    pallas_call x1, Pallas kernels: 97.3 us -> 99.7 us  [exchange(): pl.pallas_call(functools.partial(exchange_kernel, count_y, count_x), out_...]
  transfers between devices with their start and end apart: 7 -> 7, of which waited for: 2 -> 2; matrix products, arithmetic and copies ran while one was open for 7% -> 7% of each run, Pallas kernels for 69% -> 71%
where the time goes in v5:
time: 169 us; the launch traced here: 168 us
  Pallas kernels  120 us (71%)
  starting transfers between devices  22.4 us (13%)
  local copies, waits for them, and re-layouts  15.2 us (9%)
  waiting for transfers between devices  5.5 us (3%)
  other arithmetic  3.19 us (2%)
    pallas_call x1, Pallas kernels, exchange(): pl.pallas_call(functools.partial(exchange_kernel, count_y, count_x), out_...  99.7 us
    ppermute x6, starting transfers between devices, shifted(): lax.ppermute(value, axis, [(source, source + steps) for source in range(f...  12.5 us
    all_to_all x1, starting transfers between devices, per_device(): lax.all_to_all(send_quads, 'tx', split_axis=0, concat_axis=0, tiled=True)  9.85 us
    unnamed x20, local copies, waits for them, and re-layouts  7.44 us
    pallas_call x1, Pallas kernels, make_pieces(): pl.pallas_call(pieces_kernel, out_shape=jax.ShapeDtypeStruct((rows, SIDE,...  7.14 us
    pallas_call x1, Pallas kernels, join(): pl.pallas_call(join_kernel, out_shape=[jax.ShapeDtypeStruct((SLOTS, SIDE,...  6.13 us
    ppermute x6, waiting for transfers between devices, shifted(): lax.ppermute(value, axis, [(source, source + steps) for source in range(f...  5.5 us
    pallas_call x1, Pallas kernels, phase_surfaces(): pl.pallas_call(phase_kernel, out_shape=[jax.ShapeDtypeStruct((16, columns...  3.94 us
  transfers between devices with their start and end apart: 7, of which 2 were waited for; matrix products, arithmetic and copies ran while one was open for 7% of the time, Pallas kernels for 71%

profile of v5, /device:TPU:0, one launch (start us, length us, event | category | flops | bytes accessed | tf_op | source)
XLA Modules:
  0.0 168.3 jit_solution(17849379698638842513)
XLA Ops:
  0.6 0.0 copy-start.6
  0.6 0.0 copy-start.7
  0.7 0.8 fusion.26
  1.4 2.3 %collective-permute-start = (bf16[4,8,512]{2,1,0:T(8,128)(2,1)S(1)}, bf16[4,8,512]{2,1,0:T(8,128)(2,1)S(1)}, u32[]{:S(2)}, u32[]{:S(2)}) collective-permute-start(bf16[4,8,512]{2,1,0:T(8,128)(2,1)S(1)} %get-tuple-element.43), channel_id=1, source_target_pairs={{0,8},{8,16},{16,24},{1,9},{9,17},{17,25},{2,10},{10,18},{18,26},{... | collective-permute-start | bytes 98312 | tf_op jit(solution)/shard_map/ppermute | solution.py:25
  3.8 1.3 collective-permute-start.1
  5.1 3.2 %bins.1 = (f32[12,128]{1,0:T(8,128)}, f32[12,128]{1,0:T(8,128)}, f32[12,128]{1,0:T(8,128)}, f32[12,128]{1,0:T(8,128)}) custom-call(bf16[4,512,512]{2,1,0:T(8,128)(2,1)} %bitcast.38), custom_call_target="tpu_custom_call" | custom-call | flops 100000000 | bytes 2097152 | tf_op jit(solution)/shard_map/bins/pallas_call | solution.py:68
  8.3 1.4 collective-permute-start.4
  9.7 1.3 collective-permute-start.5
  11.0 1.4 fusion.25
  12.5 0.9 sine_multiply_fusion
  13.4 0.0 copy-done.6
  13.4 0.2 convert_reduce_fusion
  13.6 0.2 select_reduce_fusion
  13.8 0.1 tile.2
  13.9 0.3 mul.122
  14.1 0.1 copy.34
  14.2 0.0 copy-done.7
  14.2 0.2 convert_reduce_fusion.2
  14.4 1.4 multiply_convert_fusion.patch_ref
  15.8 0.1 cosine_multiply_fusion.1
  15.9 0.2 copy.30
  16.0 0.2 copy.32
  16.2 0.1 add.159
  16.4 0.0 collective-permute-done
  16.4 0.0 collective-permute-done.1
  16.4 0.1 fusion.28
  16.5 0.1 copy.31
  16.6 4.9 %collective-permute-start.2 = (bf16[4,8,528]{2,1,0:T(8,128)(2,1)S(1)}, bf16[4,8,528]{2,1,0:T(8,128)(2,1)S(1)}, u32[]{:S(2)}, u32[]{:S(2)}) collective-permute-start(bf16[4,8,528]{2,1,0:T(8,128)(2,1)S(1)} %maximum_bitcast_fusion), channel_id=1, source_target_pairs={{0,1},{1,2},{2,3},{3,4},{4,5},{5,6},{6,7},{8,9},{9,10},{10,11},{11... | collective-permute-start | bytes 101384 | tf_op jit(solution)/shard_map/ppermute | solution.py:25
  21.5 0.1 copy.33
  21.6 1.3 collective-permute-start.3
  22.9 0.3 collective-permute-done.2
  23.1 5.2 %collective-permute-done.3 = bf16[4,8,528]{2,1,0:T(8,128)(2,1)S(1)} collective-permute-done((bf16[4,8,528]{2,1,0:T(8,128)(2,1)S(1)}, bf16[4,8,528]{2,1,0:T(8,128)(2,1)S(1)}, u32[]{:S(2)}, u32[]{:S(2)}) %collective-permute-start.3) | collective-permute-done | bytes 33824 | tf_op jit(solution)/shard_map/ppermute | solution.py:25
  28.4 0.0 copy-done.3
  28.4 0.0 copy-start
  28.4 1.6 copy-done
  30.0 7.1 %pieces.1.send_ref = bf16[512,32,128]{2,1,0:T(8,128)(2,1)S(1)} custom-call(s32[2]{0:T(128)S(1)} %bitcast.42, s32[256]{0:T(256)S(1)} %multiply_add_fusion.1.pos_ref, bf16[4,512,512]{2,1,0:T(8,128)(2,1)S(1)} %bitcast.40, bf16[4,16,512]{2,1,0:T(8,128)(2,1)S(1)} %constant_dynamic-update-slice_fusion.tb_ref, bf16[4,16,512]{2,1,0:T(8,128)(2,1)S(1)} %slice.63.side_ref, ...), custom_call_target="tpu_custom_call" | custom-call | flops 2000000000 | bytes 8388608 | tf_op jit(solution)/shard_map/pieces/pallas_call | solution.py:198
  37.1 99.7 %exchange.1 = (bf16[512,32,128]{2,1,0:T(8,128)(2,1)S(1)}, s32[32,8,128]{2,1,0:T(8,128)S(1)}) custom-call(bf16[512,32,128]{2,1,0:T(8,128)(2,1)S(1)} %pieces.1.send_ref, s32[32,8,128]{2,1,0:T(8,128)S(1)} %pad.24.code_ref), custom_call_target="tpu_custom_call" | custom-call | bytes 8388608 | tf_op jit(solution)/shard_map/exchange/pallas_call | solution.py:277
  136.9 0.0 copy-start.1
  136.9 1.9 %copy-done.1 = bf16[512,32,128]{2,1,0:T(8,128)(2,1)} copy-done((bf16[512,32,128]{2,1,0:T(8,128)(2,1)}, bf16[512,32,128]{2,1,0:T(8,128)(2,1)S(1)}, u32[]{:S(2)}) %copy-start.1) | copy-done | bytes 4194328
  138.9 0.1 reshape_squeeze.3
  139.0 0.1 broadcast_in_dim_reshape_squeeze.3.code_ref
  139.1 2.2 %copy-done.2 = bf16[512,32,128]{2,1,0:T(8,128)(2,1)S(1)} copy-done((bf16[512,32,128]{2,1,0:T(8,128)(2,1)S(1)}, bf16[512,32,128]{2,1,0:T(8,128)(2,1)}, u32[]{:S(2)}) %copy-start.2) | copy-done | bytes 4194328
  141.3 6.1 %join.1 = (bf16[64,32,128]{2,1,0:T(8,128)(2,1)S(1)}, f32[512,128]{1,0:T(8,128)S(1)}) custom-call(s32[512]{0:T(512)S(1)} %add_select_fusion.2.slot_ref, s32[1,512]{1,0:T(1,128)S(1)} %broadcast_in_dim_reshape_squeeze.3.code_ref, bf16[32,256,128]{2,1,0:T(8,128)(2,1)S(1)} %multiply_convert_fusion.patch_ref, bf16[512,32,128]{2,1,0:T(8,128)(2,1)S(1)} %copy-done.2), custom_call_target="tpu_custom_call" | custom-call | flops 100000000 | bytes 8388608 | tf_op jit(solution)/shard_map/join/pallas_call | solution.py:344
  147.4 0.1 reshape.256
  147.6 0.1 broadcast_in_dim.22
  147.6 0.8 fusion
  148.4 9.9 %all-to-all-start = ((bf16[8,8,128]{2,1,0:T(8,128)(2,1)}), bf16[8,8,128]{2,1,0:T(8,128)(2,1)S(1)}, u32[]{:S(2)}, u32[]{:S(2)}) async-start(bf16[8,8,128]{2,1,0:T(8,128)(2,1)} %fusion), calls=%async_computation | async-start | bytes 32768 | tf_op jit(solution)/shard_map/all_to_all | solution.py:431
  158.3 0.1 sine_multiply_fusion.1
  158.4 0.6 pad.27.r_ref
  159.0 0.6 pad.29.b_ref
  159.6 0.6 pad.25.ca_ref
  160.2 0.6 pad.26.sa_ref
  160.8 0.0 collective-permute-done.4
  160.8 0.6 pad.28.l_ref
  161.4 0.0 collective-permute-done.5
  161.4 0.6 pad.30.t_ref
  162.0 3.9 %phase.1 = (f32[16,128]{1,0:T(8,128)}, f32[16,128]{1,0:T(8,128)}) custom-call(f32[16,16]{1,0:T(8,128)} %pad.25.ca_ref, f32[16,16]{1,0:T(8,128)} %pad.26.sa_ref, f32[128,128]{1,0:T(8,128)} %get-tuple-element.53.cb_ref, f32[128,128]{1,0:T(8,128)} %get-tuple-element.52.sb_ref, f32[16,128]{1,0:T(8,128)} %pad.27.r_ref, f32[16,128]{1,0:T(8,128)} %pad.28.l_ref, ...), custom_call_target="tpu_custom_call" | custom-call | flops 100000000 | bytes 262144 | tf_op jit(solution)/shard_map/phase/pallas_call | solution.py:116
  165.9 1.0 copy.39
  166.9 0.0 all-to-all-done
  166.9 0.2 convert_reduce_fusion.1
  167.1 0.1 convolution_convert_fusion
  167.2 0.1 convert_element_type.83
  167.4 0.2 copy.35
  167.6 0.7 copy.36
  (26 shorter events, 0.3 us)
Async XLA Ops:
  0.6 12.8 %copy-start.6 = (s32[1,1,256]{2,1,0:T(1,128)S(1)}, s32[1,1,256]{2,1,0:T(1,128)}, u32[]{:S(2)}) copy-start(s32[1,1,256]{2,1,0:T(1,128)} %param.6) | copy-start | bytes 3076
  0.6 13.6 %copy-start.7 = (s32[1,1,64]{2,1,0:T(1,128)S(1)}, s32[1,1,64]{2,1,0:T(1,128)}, u32[]{:S(2)}) copy-start(s32[1,1,64]{2,1,0:T(1,128)} %param.7) | copy-start | bytes 772
  1.4 14.9 %collective-permute-start = (bf16[4,8,512]{2,1,0:T(8,128)(2,1)S(1)}, bf16[4,8,512]{2,1,0:T(8,128)(2,1)S(1)}, u32[]{:S(2)}, u32[]{:S(2)}) collective-permute-start(bf16[4,8,512]{2,1,0:T(8,128)(2,1)S(1)} %get-tuple-element.43), channel_id=1, source_target_pairs={{0,8},{8,16},{16,24},{1,9},{9,17},{17,25},{2,10},{10,18},{18,26},{... | collective-permute-start | bytes 98312 | tf_op jit(solution)/shard_map/ppermute | solution.py:25
  3.8 12.6 %collective-permute-start.1 = (bf16[4,8,512]{2,1,0:T(8,128)(2,1)S(1)}, bf16[4,8,512]{2,1,0:T(8,128)(2,1)S(1)}, u32[]{:S(2)}, u32[]{:S(2)}) collective-permute-start(bf16[4,8,512]{2,1,0:T(8,128)(2,1)S(1)} %get-tuple-element.42), channel_id=1, source_target_pairs={{8,0},{16,8},{24,16},{9,1},{17,9},{25,17},{10,2},{18,10},{26,18},{... | collective-permute-start | bytes 98312 | tf_op jit(solution)/shard_map/ppermute | solution.py:25
  8.3 20.1 %copy-start.3 = (s32[1,1,2]{2,1,0:T(1,128)S(1)}, s32[1,1,2]{2,1,0:T(1,128)}, u32[]{:S(2)}) copy-start(s32[1,1,2]{2,1,0:T(1,128)} %param.5) | copy-start | bytes 28
  8.3 152.5 %collective-permute-start.4 = (f32[12,128]{1,0:T(8,128)}, f32[12,128]{1,0:T(8,128)S(1)}, u32[]{:S(2)}, u32[]{:S(2)}) collective-permute-start(f32[12,128]{1,0:T(8,128)} %get-tuple-element.19), channel_id=1, source_target_pairs={{1,0},{2,1},{3,2},{4,3},{5,4},{6,5},{7,6},{9,8},{10,9},{11,10},{12... | collective-permute-start | bytes 18440 | tf_op jit(solution)/shard_map/ppermute | solution.py:25
  9.7 151.7 %collective-permute-start.5 = (f32[12,128]{1,0:T(8,128)}, f32[12,128]{1,0:T(8,128)S(1)}, u32[]{:S(2)}, u32[]{:S(2)}) collective-permute-start(f32[12,128]{1,0:T(8,128)} %get-tuple-element.21), channel_id=1, source_target_pairs={{8,0},{16,8},{24,16},{9,1},{17,9},{25,17},{10,2},{18,10},{26,18},{... | collective-permute-start | bytes 18440 | tf_op jit(solution)/shard_map/ppermute | solution.py:25
  16.6 6.5 %collective-permute-start.2 = (bf16[4,8,528]{2,1,0:T(8,128)(2,1)S(1)}, bf16[4,8,528]{2,1,0:T(8,128)(2,1)S(1)}, u32[]{:S(2)}, u32[]{:S(2)}) collective-permute-start(bf16[4,8,528]{2,1,0:T(8,128)(2,1)S(1)} %maximum_bitcast_fusion), channel_id=1, source_target_pairs={{0,1},{1,2},{2,3},{3,4},{4,5},{5,6},{6,7},{8,9},{9,10},{10,11},{11... | collective-permute-start | bytes 101384 | tf_op jit(solution)/shard_map/ppermute | solution.py:25
  21.6 6.8 %collective-permute-start.3 = (bf16[4,8,528]{2,1,0:T(8,128)(2,1)S(1)}, bf16[4,8,528]{2,1,0:T(8,128)(2,1)S(1)}, u32[]{:S(2)}, u32[]{:S(2)}) collective-permute-start(bf16[4,8,528]{2,1,0:T(8,128)(2,1)S(1)} %maximum_bitcast_fusion.1), channel_id=1, source_target_pairs={{1,0},{2,1},{3,2},{4,3},{5,4},{6,5},{7,6},{9,8},{10,9},{11,10},{12... | collective-permute-start | bytes 101384 | tf_op jit(solution)/shard_map/ppermute | solution.py:25
  28.4 1.6 copy-start
  136.9 2.0 %copy-start.1 = (bf16[512,32,128]{2,1,0:T(8,128)(2,1)}, bf16[512,32,128]{2,1,0:T(8,128)(2,1)S(1)}, u32[]{:S(2)}) copy-start(bf16[512,32,128]{2,1,0:T(8,128)(2,1)S(1)} %get-tuple-element.15.got_ref) | copy-start | bytes 12582916
  138.8 19.5 %copy-start.5 = (f32[12,128]{1,0:T(8,128)S(1)}, f32[12,128]{1,0:T(8,128)}, u32[]{:S(2)}) copy-start(f32[12,128]{1,0:T(8,128)} %get-tuple-element.18) | copy-start | bytes 18436
  138.8 20.1 %copy-start.4 = (f32[12,128]{1,0:T(8,128)S(1)}, f32[12,128]{1,0:T(8,128)}, u32[]{:S(2)}) copy-start(f32[12,128]{1,0:T(8,128)} %get-tuple-element.20) | copy-start | bytes 18436
  139.1 2.2 %copy-start.2 = (bf16[512,32,128]{2,1,0:T(8,128)(2,1)S(1)}, bf16[512,32,128]{2,1,0:T(8,128)(2,1)}, u32[]{:S(2)}) copy-start(bf16[512,32,128]{2,1,0:T(8,128)(2,1)} %copy-done.1) | copy-start | bytes 12582916
  148.4 18.5 %all-to-all-start = ((bf16[8,8,128]{2,1,0:T(8,128)(2,1)}), bf16[8,8,128]{2,1,0:T(8,128)(2,1)S(1)}, u32[]{:S(2)}, u32[]{:S(2)}) async-start(bf16[8,8,128]{2,1,0:T(8,128)(2,1)} %fusion), calls=%async_computation | async-start | bytes 32768 | tf_op jit(solution)/shard_map/all_to_all | solution.py:431
